TPU v7x, 512 devices: a whole 4x8x8 slice. The times are simulated.
512 devices in a mesh: atoms: 128 (over z, y_hi, x, core), kpt: 4 (over y_lo).
Axes of the slice: x: 4, y: 8 (y_hi: 2, y_lo: 4; y = y_hi * 4 + y_lo), z: 8, core: 2. Of those that a mesh axis runs over, the one named last changes fastest.
Arguments:
- blocks: bfloat16 [4608, 32, 13, 13], P('atoms', 'kpt'), may hold values from -0.3125 to 0.3125
- vectors: bfloat16 [8, 4608, 2, 13, 128], P('kpt', 'atoms'), may hold values from -6 to 6
- kvecs: float32 [8, 2], replicated, may hold values from 0 to 1
- neighbours: int32 [4608, 32], P('atoms'), may hold values from 0 to 4607, as said below
- offsets: int32 [4608, 32], P('atoms'), may hold values from 0 to 48
- counts: int32 [4608], P('atoms'), may hold values from 16 to 32
Outputs:
- first: bfloat16 [8, 4608, 2, 13, 128], P('kpt', 'atoms')
- second: bfloat16 [8, 4608, 2, 13, 128], P('kpt', 'atoms')
Inputs may be any that keep to these rules, and one draw needn't show every extreme that they name: neighbours[a, s] = (a + d) mod 4608 with -32 <= d <= 32; both d = 32 and d = -32 occur.
All inputs are finite; a program needn't handle non-finite values.
Results may differ from a plain program's by a relative error of at most 0.0063.
Values may be sent and summed in bfloat16 or wider, within the bound.
No kernel may reach another device: no remote copies, remote signals or barrier semaphores. Data moves between devices by JAX's collectives and lax.ppermute only.
A program may use at most 128 MiB of HBM per device.

v0:
```python
import math

import jax
import jax.numpy as jnp
from jax import lax
from jax.sharding import PartitionSpec as P

NEIGHBOUR_REACH = 32


def extended_2(cells, sides, width):
    for axis, dim in sides:
        count = lax.axis_size(axis)
        head = lax.slice_in_dim(cells, 0, width, axis=dim)
        tail = lax.slice_in_dim(cells, cells.shape[dim] - width, cells.shape[dim], axis=dim)
        cells = jnp.concatenate(
            [
                lax.ppermute(tail, axis, [(i, (i + 1) % count) for i in range(count)]),
                cells,
                lax.ppermute(head, axis, [((i + 1) % count, i) for i in range(count)]),
            ],
            axis=dim,
        )
    return cells


def angles(kvecs, offsets):
    grid_row = (offsets // 7 - 3).astype(jnp.float32)
    grid_col = (offsets % 7 - 3).astype(jnp.float32)
    return (
        2.0
        * math.pi
        * (kvecs[:, 0, None, None] * grid_row[None] + kvecs[:, 1, None, None] * grid_col[None])
    )


def phased(kvecs, offsets, live_slot, blocks):
    theta = angles(kvecs, offsets)
    block_f = jnp.transpose(blocks, (0, 2, 1, 3)).astype(jnp.float32)[None]
    cos_part = jnp.where(live_slot[None], jnp.cos(theta), 0.0)[:, :, None, :, None]
    sin_part = jnp.where(live_slot[None], jnp.sin(theta), 0.0)[:, :, None, :, None]
    return ((cos_part * block_f).astype(jnp.bfloat16), (sin_part * block_f).astype(jnp.bfloat16))


def product(real_h, imag_h, extended, local_rows):
    slot_total = real_h.shape[3]
    group = slot_total // 4
    turns = slot_total // group
    window = extended.shape[1]
    out_shape = (real_h.shape[0], real_h.shape[1], extended.shape[2], extended.shape[3])
    window_index = jnp.arange(window, dtype=jnp.int32)

    def take_turn(running, turn_index):
        offset_row = turn_index * group
        rows_here = lax.dynamic_slice_in_dim(local_rows, offset_row, group, 1)
        selector = (rows_here[:, :, None] == window_index[None, None, :]).astype(jnp.bfloat16)
        real_g = lax.dynamic_slice_in_dim(real_h, offset_row, group, 3)
        imag_g = lax.dynamic_slice_in_dim(imag_h, offset_row, group, 3)
        upper_half = jnp.concatenate([real_g, -imag_g], axis=4)
        lower_half = jnp.concatenate([imag_g, real_g], axis=4)
        blocked = jnp.concatenate([upper_half, lower_half], axis=2)
        picked = jnp.einsum(
            "agw,kwyv->kagyv", selector, extended, preferred_element_type=jnp.float32
        ).astype(jnp.bfloat16)
        running = running + jnp.einsum(
            "kaxgy,kagyv->kaxv", blocked, picked, preferred_element_type=jnp.float32
        )
        return (running, None)

    summed, unused = lax.scan(
        take_turn, jnp.zeros(out_shape, jnp.float32), jnp.arange(turns, dtype=jnp.int32)
    )
    orbital_count = real_h.shape[2]
    return summed.astype(jnp.bfloat16).reshape(
        out_shape[0], out_shape[1], 2, orbital_count, out_shape[3]
    )


def extend(vector_block):
    margin = NEIGHBOUR_REACH
    grown = extended_2(vector_block, (("atoms", 1),), NEIGHBOUR_REACH)
    merged = grown.reshape(
        grown.shape[0], grown.shape[1], grown.shape[2] * grown.shape[3], grown.shape[4]
    )
    return (merged, margin)


def per_device(blocks, vectors, kvecs, neighbours, offsets, counts):
    atom_here = blocks.shape[0]
    slot_total = offsets.shape[1]
    owners = lax.axis_size("kpt")
    live_slot = jnp.arange(slot_total, dtype=jnp.int32)[None, :] < counts[:, None]
    slot_share = slot_total // owners
    first_slot = lax.axis_index("kpt") * slot_share
    own_offsets = lax.dynamic_slice_in_dim(offsets, first_slot, slot_share, 1)
    own_live = lax.dynamic_slice_in_dim(live_slot, first_slot, slot_share, 1)
    real_all, imag_all = phased(kvecs, own_offsets, own_live, blocks)
    real_h, imag_h = (
        lax.all_to_all(real_all, "kpt", split_axis=0, concat_axis=3, tiled=True),
        lax.all_to_all(imag_all, "kpt", split_axis=0, concat_axis=3, tiled=True),
    )
    total_atoms = atom_here * lax.axis_size("atoms")
    global_rows = lax.axis_index("atoms") * atom_here + jnp.arange(atom_here, dtype=jnp.int32)
    distance = (
        neighbours - global_rows[:, None] + total_atoms // 2
    ) % total_atoms - total_atoms // 2
    grown, margin = extend(vectors)
    local_rows = jnp.arange(atom_here, dtype=jnp.int32)[:, None] + margin + distance
    first = product(real_h, imag_h, grown, local_rows)
    grown_again, unused_margin = extend(first)
    second = product(real_h, imag_h, grown_again, local_rows)
    return (first, second)


def solution(mesh):
    placed = (
        P("atoms", "kpt", None, None),
        P("kpt", "atoms", None, None, None),
        P(),
        P("atoms", None),
        P("atoms", None),
        P("atoms"),
    )
    return jax.shard_map(
        per_device,
        mesh=mesh,
        in_specs=placed,
        out_specs=(P("kpt", "atoms", None, None, None), P("kpt", "atoms", None, None, None)),
        check_vma=False,
    )
```

profile of v0, /device:TPU:24, one launch (start us, length us, event | category | flops | bytes accessed | tf_op | source)
XLA Modules:
  0.0 329.4 jit_solution(17860794782570305147)
XLA Ops:
  4.0 2.4 multiply_convert_fusion
  6.4 6.1 %reshape.59 = bf16[4,2,48672]{2,1,0:T(2,128)(2,1)} reshape(bf16[8,13,13,8,36]{4,3,2,1,0:T(8,128)(2,1)} %bitcast.81) | data formatting | bytes 1557504
  12.5 9.0 %all-to-all-start = ((bf16[4,2,48672]{2,1,0:T(2,128)(2,1)}), bf16[4,2,48672]{2,1,0:T(2,128)(2,1)S(1)}, u32[]{:S(2)}, u32[]{:S(2)}) async-start(bf16[4,2,48672]{2,1,0:T(2,128)(2,1)} %reshape.59), calls=%async_computation | async-start | bytes 1560576 | tf_op jit(solution)/shard_map/all_to_all | solution.py:99
  21.6 4.9 %reshape.61 = bf16[4,2,48672]{2,1,0:T(2,128)(2,1)} reshape(bf16[8,13,13,8,36]{4,3,2,1,0:T(8,128)(2,1)S(1)} %bitcast.80) | data formatting | bytes 1557504
  26.5 8.8 %all-to-all-done = bf16[4,2,48672]{2,1,0:T(2,128)(2,1)S(1)} async-done(((bf16[4,2,48672]{2,1,0:T(2,128)(2,1)}), bf16[4,2,48672]{2,1,0:T(2,128)(2,1)S(1)}, u32[]{:S(2)}, u32[]{:S(2)}) %all-to-all-start) | async-done | bytes 778784 | tf_op jit(solution)/shard_map/all_to_all | solution.py:99
  35.2 6.5 %all-to-all-start.1 = ((bf16[4,2,48672]{2,1,0:T(2,128)(2,1)}), bf16[4,2,48672]{2,1,0:T(2,128)(2,1)}, u32[]{:S(2)}, u32[]{:S(2)}) async-start(bf16[4,2,48672]{2,1,0:T(2,128)(2,1)} %reshape.61), calls=%async_computation.1 | async-start | bytes 1560576 | tf_op jit(solution)/shard_map/all_to_all | solution.py:100
  43.2 1.9 collective-permute-start
  45.1 15.7 %collective-permute-start.1 = (bf16[2,32,2,13,128]{4,1,3,2,0:T(8,128)(2,1)S(1)}, bf16[2,32,2,13,128]{4,1,3,2,0:T(8,128)(2,1)S(1)}, u32[]{:S(2)}, u32[]{:S(2)}) collective-permute-start(bf16[2,32,2,13,128]{4,1,3,2,0:T(8,128)(2,1)S(1)} %get-tuple-element.218), channel_id=1, source_target_pairs={{4,0},{8,4},{12,8},{16,12},{20,16},{24,20},{28,24},{32,28},{36,32}... | collective-permute-start | bytes 1277960 | tf_op jit(solution)/shard_map/ppermute | solution.py:20
  61.6 17.1 %collective-permute-done = bf16[2,32,2,13,128]{4,1,3,2,0:T(8,128)(2,1)S(1)} collective-permute-done((bf16[2,32,2,13,128]{4,1,3,2,0:T(8,128)(2,1)S(1)}, bf16[2,32,2,13,128]{4,1,3,2,0:T(8,128)(2,1)S(1)}, u32[]{:S(2)}, u32[]{:S(2)}) %collective-permute-start) | collective-permute-done | bytes 426016 | tf_op jit(solution)/shard_map/ppermute | solution.py:18
  78.8 1.3 pad_maximum_fusion
  80.1 5.2 %reshape.60 = bf16[8,13,13,8,36]{4,3,2,1,0:T(8,128)(2,1)S(1)} reshape(bf16[4,2,48672]{2,1,0:T(2,128)(2,1)S(1)} %all-to-all-done) | data formatting | bytes 1557504
  85.3 2.0 copy.89
  87.3 19.4 %copy.53 = bf16[2,36,13,32,13]{4,2,3,1,0:T(8,128)(2,1)} copy(bf16[2,36,13,32,13]{1,3,4,2,0:T(8,128)(2,1)} %bitcast.83) | data formatting | bytes 1557504
  106.7 6.0 %reshape.62 = bf16[8,13,13,8,36]{4,3,2,1,0:T(8,128)(2,1)S(1)} reshape(bf16[4,2,48672]{2,1,0:T(2,128)(2,1)} %all-to-all-done.1) | data formatting | bytes 1557504
  112.7 2.1 copy.88
  114.7 19.3 %copy.54 = bf16[2,36,13,32,13]{4,2,3,1,0:T(8,128)(2,1)} copy(bf16[2,36,13,32,13]{1,3,4,2,0:T(8,128)(2,1)} %bitcast.85) | data formatting | bytes 1557504
  134.1 82.8 %while.22 = (s32[]{:T(128)}, f32[2,36,26,128]{3,2,1,0:T(8,128)}, s32[4]{0:T(128)S(1)}, bf16[2,36,13,32,13]{4,2,3,1,0:T(8,128)(2,1)}, bf16[2,36,13,32,13]{4,2,3,1...) while((s32[]{:T(128)}, f32[2,36,26,128]{3,2,1,0:T(8,128)}, ...), condition=%wide.region_1.2_spmd.clone, body=%wide.region_0.1_spmd.clone.sunk | while | flops 488703168 | bytes 17801812 | solution.py:70
  135.3 5.3 %fusion.79 = (bf16[2,36,13,8,13]{4,2,3,1,0:T(8,128)(2,1)S(1)}, bf16[2,36,13,8,13]{4,2,3,1,0:T(8,128)(2,1)}, bf16[2,36,13,8,13]{4,2,3,1,0:T(8,128)(2,1)}) fusion(bf16[2,36,13,32,13]{4,2,3,1,0:T(8,128)(2,1)} %get-tuple-element.353, s32[]{:T(128)S(6)} %select_n.74, bf16[2,36,13,32,13]{4,2,3,1,0:T(8,128)(2,1)} %get-tuple-element.352), kind=kLoop, calls=%fused_computation.71.clone.1 | loop fusion | flops 97344 | bytes 973444 | tf_op jit(solution)/shard_map/while/body/eval_jaxpr/neg | solution.py:59
  140.7 3.1 convert_bitcast_fusion.5
  143.9 10.8 %fusion.80 = f32[2,36,26,128]{3,2,1,0:T(8,128)} fusion(bf16[2,36,8,26,128]{4,2,3,0,1:T(8,128)(2,1)} %convert_bitcast_fusion.5, bf16[2,36,13,8,13]{4,2,3,1,0:T(8,128)(2,1)} %get-tuple-element.314, bf16[2,36,13,8,13]{4,2,3,1,0:T(8,128)(2,1)} %get-tuple-element.315, bf16[2,36,13,8,13]{4,2,3,1,0:T(8,128)(2,1)S(1)} %get-tuple-element.316, ...), kind=kOutput, calls=%fused_computation.13.clone.1 | convolution fusion | flops 103274496 | bytes 6334849 | tf_op jit(solution)/shard_map/while/body/eval_jaxpr/kaxgy,kagyv->kaxv/dot_general | solution.py:65
  155.9 5.3 %fusion.79 = (bf16[2,36,13,8,13]{4,2,3,1,0:T(8,128)(2,1)S(1)}, bf16[2,36,13,8,13]{4,2,3,1,0:T(8,128)(2,1)}, bf16[2,36,13,8,13]{4,2,3,1,0:T(8,128)(2,1)}) fusion(bf16[2,36,13,32,13]{4,2,3,1,0:T(8,128)(2,1)} %get-tuple-element.353, s32[]{:T(128)S(6)} %select_n.74, bf16[2,36,13,32,13]{4,2,3,1,0:T(8,128)(2,1)} %get-tuple-element.352), kind=kLoop, calls=%fused_computation.71.clone.1 | loop fusion | flops 97344 | bytes 973444 | tf_op jit(solution)/shard_map/while/body/eval_jaxpr/neg | solution.py:59
  161.3 3.1 convert_bitcast_fusion.5
  164.4 11.0 %fusion.80 = f32[2,36,26,128]{3,2,1,0:T(8,128)} fusion(bf16[2,36,8,26,128]{4,2,3,0,1:T(8,128)(2,1)} %convert_bitcast_fusion.5, bf16[2,36,13,8,13]{4,2,3,1,0:T(8,128)(2,1)} %get-tuple-element.314, bf16[2,36,13,8,13]{4,2,3,1,0:T(8,128)(2,1)} %get-tuple-element.315, bf16[2,36,13,8,13]{4,2,3,1,0:T(8,128)(2,1)S(1)} %get-tuple-element.316, ...), kind=kOutput, calls=%fused_computation.13.clone.1 | convolution fusion | flops 103274496 | bytes 6334849 | tf_op jit(solution)/shard_map/while/body/eval_jaxpr/kaxgy,kagyv->kaxv/dot_general | solution.py:65
  176.6 5.3 %fusion.79 = (bf16[2,36,13,8,13]{4,2,3,1,0:T(8,128)(2,1)S(1)}, bf16[2,36,13,8,13]{4,2,3,1,0:T(8,128)(2,1)}, bf16[2,36,13,8,13]{4,2,3,1,0:T(8,128)(2,1)}) fusion(bf16[2,36,13,32,13]{4,2,3,1,0:T(8,128)(2,1)} %get-tuple-element.353, s32[]{:T(128)S(6)} %select_n.74, bf16[2,36,13,32,13]{4,2,3,1,0:T(8,128)(2,1)} %get-tuple-element.352), kind=kLoop, calls=%fused_computation.71.clone.1 | loop fusion | flops 97344 | bytes 973444 | tf_op jit(solution)/shard_map/while/body/eval_jaxpr/neg | solution.py:59
  182.0 3.1 convert_bitcast_fusion.5
  185.2 11.0 %fusion.80 = f32[2,36,26,128]{3,2,1,0:T(8,128)} fusion(bf16[2,36,8,26,128]{4,2,3,0,1:T(8,128)(2,1)} %convert_bitcast_fusion.5, bf16[2,36,13,8,13]{4,2,3,1,0:T(8,128)(2,1)} %get-tuple-element.314, bf16[2,36,13,8,13]{4,2,3,1,0:T(8,128)(2,1)} %get-tuple-element.315, bf16[2,36,13,8,13]{4,2,3,1,0:T(8,128)(2,1)S(1)} %get-tuple-element.316, ...), kind=kOutput, calls=%fused_computation.13.clone.1 | convolution fusion | flops 103274496 | bytes 6334849 | tf_op jit(solution)/shard_map/while/body/eval_jaxpr/kaxgy,kagyv->kaxv/dot_general | solution.py:65
  197.4 5.3 %fusion.79 = (bf16[2,36,13,8,13]{4,2,3,1,0:T(8,128)(2,1)S(1)}, bf16[2,36,13,8,13]{4,2,3,1,0:T(8,128)(2,1)}, bf16[2,36,13,8,13]{4,2,3,1,0:T(8,128)(2,1)}) fusion(bf16[2,36,13,32,13]{4,2,3,1,0:T(8,128)(2,1)} %get-tuple-element.353, s32[]{:T(128)S(6)} %select_n.74, bf16[2,36,13,32,13]{4,2,3,1,0:T(8,128)(2,1)} %get-tuple-element.352), kind=kLoop, calls=%fused_computation.71.clone.1 | loop fusion | flops 97344 | bytes 973444 | tf_op jit(solution)/shard_map/while/body/eval_jaxpr/neg | solution.py:59
  202.8 3.1 convert_bitcast_fusion.5
  205.9 11.0 %fusion.80 = f32[2,36,26,128]{3,2,1,0:T(8,128)} fusion(bf16[2,36,8,26,128]{4,2,3,0,1:T(8,128)(2,1)} %convert_bitcast_fusion.5, bf16[2,36,13,8,13]{4,2,3,1,0:T(8,128)(2,1)} %get-tuple-element.314, bf16[2,36,13,8,13]{4,2,3,1,0:T(8,128)(2,1)} %get-tuple-element.315, bf16[2,36,13,8,13]{4,2,3,1,0:T(8,128)(2,1)S(1)} %get-tuple-element.316, ...), kind=kOutput, calls=%fused_computation.13.clone.1 | convolution fusion | flops 103274496 | bytes 6334849 | tf_op jit(solution)/shard_map/while/body/eval_jaxpr/kaxgy,kagyv->kaxv/dot_general | solution.py:65
  216.8 2.1 copy.87
  219.4 1.9 collective-permute-start.2
  221.3 11.8 %collective-permute-start.3 = (bf16[2,32,2,13,128]{4,0,3,2,1:T(2,128)(2,1)S(1)}, bf16[2,32,2,13,128]{4,0,3,2,1:T(2,128)(2,1)S(1)}, u32[]{:S(2)}, u32[]{:S(2)}) collective-permute-start(bf16[2,32,2,13,128]{4,0,3,2,1:T(2,128)(2,1)S(1)} %get-tuple-element.220), channel_id=1, source_target_pairs={{4,0},{8,4},{12,8},{16,12},{20,16},{24,20},{28,24},{32,28},{36,32}... | collective-permute-start | bytes 1277960 | tf_op jit(solution)/shard_map/ppermute | solution.py:20
  234.3 5.8 %collective-permute-done.2 = bf16[2,32,2,13,128]{4,0,3,2,1:T(2,128)(2,1)S(1)} collective-permute-done((bf16[2,32,2,13,128]{4,0,3,2,1:T(2,128)(2,1)S(1)}, bf16[2,32,2,13,128]{4,0,3,2,1:T(2,128)(2,1)S(1)}, u32[]{:S(2)}, u32[]{:S(2)}) %collective-permute-start.2) | collective-permute-done | bytes 426016 | tf_op jit(solution)/shard_map/ppermute | solution.py:18
  240.0 2.2 pad_maximum_fusion.1
  243.5 82.8 %while.23 = (s32[]{:T(128)}, f32[2,36,26,128]{3,2,1,0:T(8,128)}, s32[4]{0:T(128)S(1)}, bf16[2,36,13,32,13]{4,2,3,1,0:T(8,128)(2,1)}, bf16[2,36,13,32,13]{4,2,3,1...) while((s32[]{:T(128)}, f32[2,36,26,128]{3,2,1,0:T(8,128)}, ...), condition=%wide.region_3.4_spmd.clone, body=%wide.region_2.3_spmd.clone.sunk | while | flops 488703168 | bytes 17801812 | solution.py:70
  244.8 5.3 %fusion.85 = (bf16[2,36,13,8,13]{4,2,3,1,0:T(8,128)(2,1)S(1)}, bf16[2,36,13,8,13]{4,2,3,1,0:T(8,128)(2,1)}, bf16[2,36,13,8,13]{4,2,3,1,0:T(8,128)(2,1)}) fusion(bf16[2,36,13,32,13]{4,2,3,1,0:T(8,128)(2,1)} %get-tuple-element.386, s32[]{:T(128)S(6)} %select_n.75, bf16[2,36,13,32,13]{4,2,3,1,0:T(8,128)(2,1)} %get-tuple-element.385), kind=kLoop, calls=%fused_computation.72.clone.1 | loop fusion | flops 97344 | bytes 973444 | tf_op jit(solution)/shard_map/while/body/eval_jaxpr/neg | solution.py:59
  250.2 3.1 convert_bitcast_fusion.6
  253.3 10.8 %fusion.86 = f32[2,36,26,128]{3,2,1,0:T(8,128)} fusion(bf16[2,36,8,26,128]{4,2,3,0,1:T(8,128)(2,1)} %convert_bitcast_fusion.6, bf16[2,36,13,8,13]{4,2,3,1,0:T(8,128)(2,1)} %get-tuple-element.324, bf16[2,36,13,8,13]{4,2,3,1,0:T(8,128)(2,1)} %get-tuple-element.325, bf16[2,36,13,8,13]{4,2,3,1,0:T(8,128)(2,1)S(1)} %get-tuple-element.326, ...), kind=kOutput, calls=%fused_computation.33.clone.1 | convolution fusion | flops 103274496 | bytes 6334849 | tf_op jit(solution)/shard_map/while/body/eval_jaxpr/kaxgy,kagyv->kaxv/dot_general | solution.py:65
  265.4 5.3 %fusion.85 = (bf16[2,36,13,8,13]{4,2,3,1,0:T(8,128)(2,1)S(1)}, bf16[2,36,13,8,13]{4,2,3,1,0:T(8,128)(2,1)}, bf16[2,36,13,8,13]{4,2,3,1,0:T(8,128)(2,1)}) fusion(bf16[2,36,13,32,13]{4,2,3,1,0:T(8,128)(2,1)} %get-tuple-element.386, s32[]{:T(128)S(6)} %select_n.75, bf16[2,36,13,32,13]{4,2,3,1,0:T(8,128)(2,1)} %get-tuple-element.385), kind=kLoop, calls=%fused_computation.72.clone.1 | loop fusion | flops 97344 | bytes 973444 | tf_op jit(solution)/shard_map/while/body/eval_jaxpr/neg | solution.py:59
  270.8 3.1 convert_bitcast_fusion.6
  273.9 11.0 %fusion.86 = f32[2,36,26,128]{3,2,1,0:T(8,128)} fusion(bf16[2,36,8,26,128]{4,2,3,0,1:T(8,128)(2,1)} %convert_bitcast_fusion.6, bf16[2,36,13,8,13]{4,2,3,1,0:T(8,128)(2,1)} %get-tuple-element.324, bf16[2,36,13,8,13]{4,2,3,1,0:T(8,128)(2,1)} %get-tuple-element.325, bf16[2,36,13,8,13]{4,2,3,1,0:T(8,128)(2,1)S(1)} %get-tuple-element.326, ...), kind=kOutput, calls=%fused_computation.33.clone.1 | convolution fusion | flops 103274496 | bytes 6334849 | tf_op jit(solution)/shard_map/while/body/eval_jaxpr/kaxgy,kagyv->kaxv/dot_general | solution.py:65
  286.1 5.3 %fusion.85 = (bf16[2,36,13,8,13]{4,2,3,1,0:T(8,128)(2,1)S(1)}, bf16[2,36,13,8,13]{4,2,3,1,0:T(8,128)(2,1)}, bf16[2,36,13,8,13]{4,2,3,1,0:T(8,128)(2,1)}) fusion(bf16[2,36,13,32,13]{4,2,3,1,0:T(8,128)(2,1)} %get-tuple-element.386, s32[]{:T(128)S(6)} %select_n.75, bf16[2,36,13,32,13]{4,2,3,1,0:T(8,128)(2,1)} %get-tuple-element.385), kind=kLoop, calls=%fused_computation.72.clone.1 | loop fusion | flops 97344 | bytes 973444 | tf_op jit(solution)/shard_map/while/body/eval_jaxpr/neg | solution.py:59
  291.5 3.1 convert_bitcast_fusion.6
  294.6 11.0 %fusion.86 = f32[2,36,26,128]{3,2,1,0:T(8,128)} fusion(bf16[2,36,8,26,128]{4,2,3,0,1:T(8,128)(2,1)} %convert_bitcast_fusion.6, bf16[2,36,13,8,13]{4,2,3,1,0:T(8,128)(2,1)} %get-tuple-element.324, bf16[2,36,13,8,13]{4,2,3,1,0:T(8,128)(2,1)} %get-tuple-element.325, bf16[2,36,13,8,13]{4,2,3,1,0:T(8,128)(2,1)S(1)} %get-tuple-element.326, ...), kind=kOutput, calls=%fused_computation.33.clone.1 | convolution fusion | flops 103274496 | bytes 6334849 | tf_op jit(solution)/shard_map/while/body/eval_jaxpr/kaxgy,kagyv->kaxv/dot_general | solution.py:65
  306.9 5.3 %fusion.85 = (bf16[2,36,13,8,13]{4,2,3,1,0:T(8,128)(2,1)S(1)}, bf16[2,36,13,8,13]{4,2,3,1,0:T(8,128)(2,1)}, bf16[2,36,13,8,13]{4,2,3,1,0:T(8,128)(2,1)}) fusion(bf16[2,36,13,32,13]{4,2,3,1,0:T(8,128)(2,1)} %get-tuple-element.386, s32[]{:T(128)S(6)} %select_n.75, bf16[2,36,13,32,13]{4,2,3,1,0:T(8,128)(2,1)} %get-tuple-element.385), kind=kLoop, calls=%fused_computation.72.clone.1 | loop fusion | flops 97344 | bytes 973444 | tf_op jit(solution)/shard_map/while/body/eval_jaxpr/neg | solution.py:59
  312.2 3.1 convert_bitcast_fusion.6
  315.4 11.0 %fusion.86 = f32[2,36,26,128]{3,2,1,0:T(8,128)} fusion(bf16[2,36,8,26,128]{4,2,3,0,1:T(8,128)(2,1)} %convert_bitcast_fusion.6, bf16[2,36,13,8,13]{4,2,3,1,0:T(8,128)(2,1)} %get-tuple-element.324, bf16[2,36,13,8,13]{4,2,3,1,0:T(8,128)(2,1)} %get-tuple-element.325, bf16[2,36,13,8,13]{4,2,3,1,0:T(8,128)(2,1)S(1)} %get-tuple-element.326, ...), kind=kOutput, calls=%fused_computation.33.clone.1 | convolution fusion | flops 103274496 | bytes 6334849 | tf_op jit(solution)/shard_map/while/body/eval_jaxpr/kaxgy,kagyv->kaxv/dot_general | solution.py:65
  326.3 1.4 convert_element_type.45
  (58 shorter events, 15.5 us)
Async XLA Ops:
  12.5 22.7 %all-to-all-start = ((bf16[4,2,48672]{2,1,0:T(2,128)(2,1)}), bf16[4,2,48672]{2,1,0:T(2,128)(2,1)S(1)}, u32[]{:S(2)}, u32[]{:S(2)}) async-start(bf16[4,2,48672]{2,1,0:T(2,128)(2,1)} %reshape.59), calls=%async_computation | async-start | bytes 1560576 | tf_op jit(solution)/shard_map/all_to_all | solution.py:99
  26.5 34.3 %copy-start.3 = (s32[36,32]{0,1:T(8,128)S(1)}, s32[36,32]{0,1:T(8,128)}, u32[]{:S(2)}) copy-start(s32[36,32]{0,1:T(8,128)} %param.13) | copy-start | bytes 13828
  35.2 71.4 %all-to-all-start.1 = ((bf16[4,2,48672]{2,1,0:T(2,128)(2,1)}), bf16[4,2,48672]{2,1,0:T(2,128)(2,1)}, u32[]{:S(2)}, u32[]{:S(2)}) async-start(bf16[4,2,48672]{2,1,0:T(2,128)(2,1)} %reshape.61), calls=%async_computation.1 | async-start | bytes 1560576 | tf_op jit(solution)/shard_map/all_to_all | solution.py:100
  43.2 35.6 %collective-permute-start = (bf16[2,32,2,13,128]{4,1,3,2,0:T(8,128)(2,1)S(1)}, bf16[2,32,2,13,128]{4,1,3,2,0:T(8,128)(2,1)S(1)}, u32[]{:S(2)}, u32[]{:S(2)}) collective-permute-start(bf16[2,32,2,13,128]{4,1,3,2,0:T(8,128)(2,1)S(1)} %get-tuple-element.217), channel_id=1, source_target_pairs={{0,4},{4,8},{8,12},{12,16},{16,20},{20,24},{24,28},{28,32},{32,36}... | collective-permute-start | bytes 1277960 | tf_op jit(solution)/shard_map/ppermute | solution.py:18
  45.1 33.7 %collective-permute-start.1 = (bf16[2,32,2,13,128]{4,1,3,2,0:T(8,128)(2,1)S(1)}, bf16[2,32,2,13,128]{4,1,3,2,0:T(8,128)(2,1)S(1)}, u32[]{:S(2)}, u32[]{:S(2)}) collective-permute-start(bf16[2,32,2,13,128]{4,1,3,2,0:T(8,128)(2,1)S(1)} %get-tuple-element.218), channel_id=1, source_target_pairs={{4,0},{8,4},{12,8},{16,12},{20,16},{24,20},{28,24},{32,28},{36,32}... | collective-permute-start | bytes 1277960 | tf_op jit(solution)/shard_map/ppermute | solution.py:20
  114.7 19.3 %copy-start.2 = (s32[36,32]{1,0:T(8,128)S(1)}, s32[36,32]{1,0:T(8,128)}, u32[]{:S(2)}) copy-start(s32[36,32]{1,0:T(8,128)} %fusion.53) | copy-start | bytes 13828
  135.3 5.4 %copy-start = (bf16[2,100,26,128]{3,1,2,0:T(8,128)(2,1)S(1)}, bf16[2,100,26,128]{3,1,2,0:T(8,128)(2,1)}, u32[]{:S(2)}) copy-start(bf16[2,100,26,128]{3,1,2,0:T(8,128)(2,1)} %get-tuple-element.355) | copy-start | bytes 3993604 | tf_op jit(solution)/shard_map/while
  155.9 5.4 %copy-start = (bf16[2,100,26,128]{3,1,2,0:T(8,128)(2,1)S(1)}, bf16[2,100,26,128]{3,1,2,0:T(8,128)(2,1)}, u32[]{:S(2)}) copy-start(bf16[2,100,26,128]{3,1,2,0:T(8,128)(2,1)} %get-tuple-element.355) | copy-start | bytes 3993604 | tf_op jit(solution)/shard_map/while
  176.6 5.4 %copy-start = (bf16[2,100,26,128]{3,1,2,0:T(8,128)(2,1)S(1)}, bf16[2,100,26,128]{3,1,2,0:T(8,128)(2,1)}, u32[]{:S(2)}) copy-start(bf16[2,100,26,128]{3,1,2,0:T(8,128)(2,1)} %get-tuple-element.355) | copy-start | bytes 3993604 | tf_op jit(solution)/shard_map/while
  197.3 5.4 %copy-start = (bf16[2,100,26,128]{3,1,2,0:T(8,128)(2,1)S(1)}, bf16[2,100,26,128]{3,1,2,0:T(8,128)(2,1)}, u32[]{:S(2)}) copy-start(bf16[2,100,26,128]{3,1,2,0:T(8,128)(2,1)} %get-tuple-element.355) | copy-start | bytes 3993604 | tf_op jit(solution)/shard_map/while
  219.4 20.6 %collective-permute-start.2 = (bf16[2,32,2,13,128]{4,0,3,2,1:T(2,128)(2,1)S(1)}, bf16[2,32,2,13,128]{4,0,3,2,1:T(2,128)(2,1)S(1)}, u32[]{:S(2)}, u32[]{:S(2)}) collective-permute-start(bf16[2,32,2,13,128]{4,0,3,2,1:T(2,128)(2,1)S(1)} %get-tuple-element.219), channel_id=1, source_target_pairs={{0,4},{4,8},{8,12},{12,16},{16,20},{20,24},{24,28},{28,32},{32,36}... | collective-permute-start | bytes 1277960 | tf_op jit(solution)/shard_map/ppermute | solution.py:18
  221.3 18.7 %collective-permute-start.3 = (bf16[2,32,2,13,128]{4,0,3,2,1:T(2,128)(2,1)S(1)}, bf16[2,32,2,13,128]{4,0,3,2,1:T(2,128)(2,1)S(1)}, u32[]{:S(2)}, u32[]{:S(2)}) collective-permute-start(bf16[2,32,2,13,128]{4,0,3,2,1:T(2,128)(2,1)S(1)} %get-tuple-element.220), channel_id=1, source_target_pairs={{4,0},{8,4},{12,8},{16,12},{20,16},{24,20},{28,24},{32,28},{36,32}... | collective-permute-start | bytes 1277960 | tf_op jit(solution)/shard_map/ppermute | solution.py:20
  244.8 5.4 %copy-start.1 = (bf16[2,100,26,128]{3,1,2,0:T(8,128)(2,1)S(1)}, bf16[2,100,26,128]{3,1,2,0:T(8,128)(2,1)}, u32[]{:S(2)}) copy-start(bf16[2,100,26,128]{3,1,2,0:T(8,128)(2,1)} %get-tuple-element.388) | copy-start | bytes 3993604 | tf_op jit(solution)/shard_map/while
  265.4 5.4 %copy-start.1 = (bf16[2,100,26,128]{3,1,2,0:T(8,128)(2,1)S(1)}, bf16[2,100,26,128]{3,1,2,0:T(8,128)(2,1)}, u32[]{:S(2)}) copy-start(bf16[2,100,26,128]{3,1,2,0:T(8,128)(2,1)} %get-tuple-element.388) | copy-start | bytes 3993604 | tf_op jit(solution)/shard_map/while
  286.1 5.4 %copy-start.1 = (bf16[2,100,26,128]{3,1,2,0:T(8,128)(2,1)S(1)}, bf16[2,100,26,128]{3,1,2,0:T(8,128)(2,1)}, u32[]{:S(2)}) copy-start(bf16[2,100,26,128]{3,1,2,0:T(8,128)(2,1)} %get-tuple-element.388) | copy-start | bytes 3993604 | tf_op jit(solution)/shard_map/while
  306.8 5.4 %copy-start.1 = (bf16[2,100,26,128]{3,1,2,0:T(8,128)(2,1)S(1)}, bf16[2,100,26,128]{3,1,2,0:T(8,128)(2,1)}, u32[]{:S(2)}) copy-start(bf16[2,100,26,128]{3,1,2,0:T(8,128)(2,1)} %get-tuple-element.388) | copy-start | bytes 3993604 | tf_op jit(solution)/shard_map/while
where the time goes:
time: 330 us; the launch traced here: 329 us
  matrix products  112 us (34%)
  local copies, waits for them, and re-layouts  79.2 us (24%)
  other arithmetic  53.2 us (16%)
  starting transfers between devices  46.9 us (14%)
  waiting for transfers between devices  31.7 us (10%)
  loops' own time  5.27 us (2%)
    dot_general x8, matrix products, take_turn(): jnp.einsum('kaxgy,kagyv->kaxv', blocked, picked, preferred_element_type=j...  87.3 us
    unnamed x15, local copies, waits for them, and re-layouts  65.7 us
    neg x8, other arithmetic, take_turn(): upper_half = jnp.concatenate([real_g, -imag_g], axis=4)  42.6 us
    ppermute x2, starting transfers between devices, extended_2(): lax.ppermute(head, axis, [((i + 1) % count, i) for i in range(count)])  27.5 us
    dot_general x8, matrix products, take_turn(): jnp.einsum('agw,kwyv->kagyv', selector, extended, preferred_element_type=...  25 us
    ppermute x2, waiting for transfers between devices, extended_2(): lax.ppermute(tail, axis, [(i, (i + 1) % count) for i in range(count)])  22.9 us
    all_to_all x1, starting transfers between devices, per_device(): lax.all_to_all(real_all, 'kpt', split_axis=0, concat_axis=3, tiled=True)  9.03 us
    all_to_all x1, waiting for transfers between devices, per_device(): lax.all_to_all(real_all, 'kpt', split_axis=0, concat_axis=3, tiled=True)  8.77 us
  transfers between devices with their start and end apart: 6, of which 3 were waited for; matrix products, arithmetic and copies ran while one was open for 11% of the time, Pallas kernels for 0%

commit v1 on v0

v1 whole, which is shorter than its diff:
```python
import math

import jax
import jax.numpy as jnp
from jax import lax
from jax.experimental import pallas as pl
from jax.experimental.pallas import tpu as pltpu
from jax.sharding import PartitionSpec as P

REACH = 32
NO = 13
NV = 128
SLOTS = 32
OWN = 8
LANES = 128
ROWS = 16
VMEM = pl.BlockSpec(memory_space=pltpu.VMEM)
SMEM = pl.BlockSpec(memory_space=pltpu.SMEM)


def pack_kernel(blocks_ref, out_ref, buf):
    atoms = blocks_ref.shape[3]
    buf[...] = jnp.zeros_like(buf)
    r = lax.broadcasted_iota(jnp.int32, (NO * OWN, LANES), 0)
    c = lax.broadcasted_iota(jnp.int32, (NO * OWN, LANES), 1)
    place = ((r % OWN == c // ROWS) & (r // OWN == c % ROWS)).astype(jnp.float32).astype(jnp.bfloat16)
    for x in range(NO):
        b = blocks_ref[x].astype(jnp.float32).reshape(NO * OWN, atoms).astype(jnp.bfloat16)
        t = lax.dot_general(b, place, (((0,), (0,)), ((), ())), preferred_element_type=jnp.float32)
        buf[pl.ds(x, atoms, stride=ROWS), :] = t
    out_ref[...] = buf[...].astype(jnp.bfloat16)


def pack_blocks(blocks):
    atoms = blocks.shape[0]
    return pl.pallas_call(
        pack_kernel,
        out_shape=jax.ShapeDtypeStruct((atoms * ROWS, LANES), jnp.bfloat16),
        in_specs=[VMEM],
        out_specs=VMEM,
        scratch_shapes=[pltpu.VMEM((atoms * ROWS, LANES), jnp.float32)],
        name="pack_blocks",
    )(jnp.transpose(blocks, (2, 3, 1, 0)))


def phase_kernel(kv_ref, spot_ref, offs_ref, counts_ref, b0, b1, b2, b3, h_ref, ce, se):
    atoms = offs_ref.shape[1]
    nk = h_ref.shape[0] // (atoms * 2 * ROWS)
    mine = spot_ref[0]
    offs = offs_ref[...]
    g0 = (offs // 7 - 3).astype(jnp.float32)
    g1 = (offs % 7 - 3).astype(jnp.float32)
    slot = lax.broadcasted_iota(jnp.int32, offs.shape, 0)
    live = slot < counts_ref[...]
    width = 4 * LANES
    r = lax.broadcasted_iota(jnp.int32, (SLOTS, width), 0)
    c = lax.broadcasted_iota(jnp.int32, (SLOTS, width), 1)
    group = (c // LANES + mine) % 4
    spread = (r == group * OWN + (c % LANES) // ROWS).astype(jnp.float32)
    for k in range(nk):
        theta = (2.0 * math.pi) * (kv_ref[nk * mine + k, 0] * g0 + kv_ref[nk * mine + k, 1] * g1)
        for dst, val in ((ce, jnp.cos(theta)), (se, jnp.sin(theta))):
            wide = lax.dot_general(
                jnp.where(live, val, 0.0), spread, (((0,), (0,)), ((), ())),
                precision=lax.Precision.HIGHEST, preferred_element_type=jnp.float32)
            for g in range(4):
                top = (g * nk + k) * atoms
                dst[top:top + atoms, :] = wide[:, g * LANES:(g + 1) * LANES]
    pieces = (b0, b1, b2, b3)

    def one(a, carry):
        for g in range(4):
            lanes = slice(g * LANES, (g + 1) * LANES)
            block = pieces[g][pl.ds(pl.multiple_of(a * ROWS, ROWS), ROWS), :].astype(jnp.float32)
            for k in range(nk):
                row = pl.multiple_of((k * atoms + a) * 2 * ROWS, 2 * ROWS)
                h_ref[pl.ds(row, ROWS), lanes] = (ce[pl.ds((g * nk + k) * atoms + a, 1), :] * block).astype(jnp.bfloat16)
                h_ref[pl.ds(row + ROWS, ROWS), lanes] = (se[pl.ds((g * nk + k) * atoms + a, 1), :] * block).astype(jnp.bfloat16)
        return carry

    lax.fori_loop(0, atoms, one, 0)


def phase_blocks(kvecs, spot, offsets, counts, pieces, nk):
    atoms = offsets.shape[0]
    return pl.pallas_call(
        phase_kernel,
        out_shape=jax.ShapeDtypeStruct((nk * atoms * 2 * ROWS, 4 * LANES), jnp.bfloat16),
        in_specs=[SMEM, SMEM] + [VMEM] * 6,
        out_specs=VMEM,
        scratch_shapes=[pltpu.VMEM((4 * nk * atoms, LANES), jnp.float32)] * 2,
        name="phase_blocks",
    )(kvecs, spot, offsets.T, counts.reshape(1, atoms), *pieces)


def apply_kernel(nbr_ref, spot_ref, h_ref, own_ref, left_ref, right_ref, *rest, halos):
    if halos:
        out_ref, tail_ref, head_ref, flat, win, acc = rest
    else:
        out_ref, flat, win, acc = rest
    atoms = nbr_ref.shape[1]
    nk = h_ref.shape[0] // (atoms * 2 * ROWS)
    window = atoms + 2 * REACH
    edge = REACH * 2 * NO
    mid = atoms * 2 * NO
    span = edge * 2 + mid
    mine = spot_ref[0]
    for k in range(nk):
        flat[k * span:k * span + edge, :] = left_ref[k * edge:(k + 1) * edge, :].astype(jnp.float32)
        flat[k * span + edge:k * span + edge + mid, :] = own_ref[k * mid:(k + 1) * mid, :].astype(jnp.float32)
        flat[k * span + edge + mid:(k + 1) * span, :] = right_ref[k * edge:(k + 1) * edge, :].astype(jnp.float32)
    flat[nk * span:, :] = jnp.zeros((flat.shape[0] - nk * span, NV), jnp.float32)

    def split(i, carry):
        for j in range(4):
            w = i * 4 + j
            for part in range(2):
                win[w, part] = flat[pl.ds(w * 2 * NO + part, ROWS, stride=2), :].astype(jnp.bfloat16)
        return carry

    lax.fori_loop(0, nk * window // 4, split, 0)

    def one(a, carry):
        for k in range(nk):
            row = pl.multiple_of((k * atoms + a) * 2 * ROWS, 2 * ROWS)
            total = None
            for half in range(2):
                tiles = []
                for g in (2 * half, 2 * half + 1):
                    base = ((mine + g) % 4) * OWN
                    for s in range(OWN):
                        w = nbr_ref[base + s, a] + k * window
                        tiles.append(jnp.concatenate([win[w, 0], win[w, 1]], axis=1))
                rhs = jnp.concatenate(tiles, axis=0)
                lhs = h_ref[pl.ds(row, 2 * ROWS), 2 * half * LANES:(2 * half + 2) * LANES]
                got = jnp.dot(lhs, rhs, preferred_element_type=jnp.float32)
                total = got if total is None else total + got
            re = total[:ROWS, :NV] - total[ROWS:, NV:]
            im = total[:ROWS, NV:] + total[ROWS:, :NV]
            start = (k * atoms + a) * 2 * NO
            acc[pl.ds(start, NO, stride=2), :] = re[:NO]
            acc[pl.ds(start + 1, NO, stride=2), :] = im[:NO]
        return carry

    lax.fori_loop(0, atoms, one, 0)
    for k in range(nk):
        base = k * mid
        out_ref[base:base + mid, :] = acc[base:base + mid, :].astype(jnp.bfloat16)
        if halos:
            tail_ref[k * edge:(k + 1) * edge, :] = acc[base + mid - edge:base + mid, :].astype(jnp.bfloat16)
            head_ref[k * edge:(k + 1) * edge, :] = acc[base:base + edge, :].astype(jnp.bfloat16)


def apply_blocks(nbr, spot, h, own, left, right, halos):
    atoms = nbr.shape[1]
    nk = h.shape[0] // (atoms * 2 * ROWS)
    edge = nk * REACH * 2 * NO
    window = atoms + 2 * REACH
    shapes = [jax.ShapeDtypeStruct(own.shape, jnp.bfloat16)]
    if halos:
        shapes += [jax.ShapeDtypeStruct((edge, NV), jnp.bfloat16)] * 2
    return pl.pallas_call(
        lambda *refs: apply_kernel(*refs, halos=halos),
        out_shape=shapes,
        in_specs=[SMEM, SMEM] + [VMEM] * 4,
        out_specs=[VMEM] * len(shapes),
        scratch_shapes=[
            pltpu.VMEM((nk * window * 2 * NO + ROWS, NV), jnp.float32),
            pltpu.VMEM((nk * window, 2, ROWS, NV), jnp.bfloat16),
            pltpu.VMEM((own.shape[0], NV), jnp.float32),
        ],
        name="apply_blocks",
    )(nbr, spot, h, own, left, right)


def exchange(tail, head):
    n = lax.axis_size("atoms")
    left = lax.ppermute(tail, "atoms", [(i, (i + 1) % n) for i in range(n)])
    right = lax.ppermute(head, "atoms", [((i + 1) % n, i) for i in range(n)])
    return left, right


def per_device(blocks, vectors, kvecs, neighbours, offsets, counts):
    atoms = blocks.shape[0]
    nk = vectors.shape[0]
    rows = jnp.transpose(vectors, (0, 1, 3, 2, 4)).reshape(nk * atoms * NO * 2, NV)
    per_k = rows.reshape(nk, atoms * NO * 2, NV)
    edge = REACH * NO * 2
    left, right = exchange(per_k[:, -edge:].reshape(nk * edge, NV), per_k[:, :edge].reshape(nk * edge, NV))
    packed = pack_blocks(blocks)
    owners = lax.axis_size("kpt")
    pieces = [packed] + [
        lax.ppermute(packed, "kpt", [(i, (i - d) % owners) for i in range(owners)]) for d in range(1, owners)
    ]
    spot = lax.axis_index("kpt").astype(jnp.int32).reshape(1)
    total_atoms = atoms * lax.axis_size("atoms")
    base = lax.axis_index("atoms") * atoms - REACH
    nbr = (neighbours.T - base + total_atoms) % total_atoms
    h = phase_blocks(kvecs, spot, offsets, counts, pieces, nk)
    first, tail, head = apply_blocks(nbr, spot, h, rows, left, right, True)
    left, right = exchange(tail, head)
    (second,) = apply_blocks(nbr, spot, h, first, left, right, False)

    def whole(flat):
        return jnp.transpose(flat.reshape(nk, atoms, NO, 2, NV), (0, 1, 3, 2, 4))

    return whole(first), whole(second)


def solution(mesh):
    placed = (
        P("atoms", "kpt", None, None),
        P("kpt", "atoms", None, None, None),
        P(),
        P("atoms", None),
        P("atoms", None),
        P("atoms"),
    )
    return jax.shard_map(
        per_device,
        mesh=mesh,
        in_specs=placed,
        out_specs=(P("kpt", "atoms", None, None, None), P("kpt", "atoms", None, None, None)),
        check_vma=False,
    )
```

time: 330 us -> 95.8 us (0.29)
  the two profiles are of different devices: /device:TPU:24 before, /device:TPU:255 now
where the time goes in v1:
time: 95.8 us; the launch traced here: 95.4 us
  starting transfers between devices  31.3 us (33%)
  waiting for transfers between devices  29 us (30%)
  Pallas kernels  28.1 us (29%)
  local copies, waits for them, and re-layouts  5 us (5%)
  other arithmetic  1.33 us (1%)
    pallas_call x2, Pallas kernels, apply_blocks(): pl.pallas_call(lambda *refs: apply_kernel(*refs, halos=halos), out_shape=...  22.4 us
    ppermute x2, starting transfers between devices, exchange(): left = lax.ppermute(tail, 'atoms', [(i, (i + 1) % n) for i in range(n)])  20.2 us
    ppermute x2, waiting for transfers between devices, exchange(): right = lax.ppermute(head, 'atoms', [((i + 1) % n, i) for i in range(n)])  13 us
    ppermute x3, waiting for transfers between devices, per_device(): lax.ppermute(packed, 'kpt', [(i, (i - d) % owners) for i in range(owners)])  9.01 us
    ppermute x3, starting transfers between devices, per_device(): lax.ppermute(packed, 'kpt', [(i, (i - d) % owners) for i in range(owners)])  7.23 us
    ppermute x2, waiting for transfers between devices, exchange(): left = lax.ppermute(tail, 'atoms', [(i, (i + 1) % n) for i in range(n)])  6.93 us
    ppermute x2, starting transfers between devices, exchange(): right = lax.ppermute(head, 'atoms', [((i + 1) % n, i) for i in range(n)])  3.84 us
    pallas_call x1, Pallas kernels, phase_blocks(): pl.pallas_call(phase_kernel, out_shape=jax.ShapeDtypeStruct((nk * atoms *...  3.79 us
  transfers between devices with their start and end apart: 7, of which 4 were waited for; matrix products, arithmetic and copies ran while one was open for 3% of the time, Pallas kernels for 6%

profile of v1, /device:TPU:255, one launch (start us, length us, event | category | flops | bytes accessed | tf_op | source)
XLA Modules:
  0.0 95.4 jit_solution(11286259471504158416)
XLA Ops:
  0.6 1.3 %fusion.1 = (bf16[2,832,128]{2,1,0:T(8,128)(2,1)S(1)}, bf16[2,832,128]{2,1,0:T(8,128)(2,1)S(1)}) fusion(bf16[2,936,128]{2,1,0:T(8,128)(2,1)} %bitcast.27), kind=kLoop, calls=%fused_computation.5 | loop fusion | bytes 1703936 | tf_op jit(solution)/shard_map/slice | solution.py:189
  1.9 7.9 %collective-permute-start.3 = (bf16[1664,128]{1,0:T(8,128)(2,1)S(1)}, bf16[1664,128]{1,0:T(8,128)(2,1)S(1)}, u32[]{:S(2)}, u32[]{:S(2)}) collective-permute-start(bf16[1664,128]{1,0:T(8,128)(2,1)S(1)} %bitcast.32), channel_id=1, source_target_pairs={{0,4},{4,8},{8,12},{12,16},{16,20},{20,24},{24,28},{28,32},{32,36}... | collective-permute-start | bytes 1277960 | tf_op jit(solution)/shard_map/ppermute | solution.py:178
  9.9 1.9 %collective-permute-start.4 = (bf16[1664,128]{1,0:T(8,128)(2,1)S(1)}, bf16[1664,128]{1,0:T(8,128)(2,1)S(1)}, u32[]{:S(2)}, u32[]{:S(2)}) collective-permute-start(bf16[1664,128]{1,0:T(8,128)(2,1)S(1)} %bitcast.31), channel_id=1, source_target_pairs={{4,0},{8,4},{12,8},{16,12},{20,16},{24,20},{28,24},{32,28},{36,32}... | collective-permute-start | bytes 1277960 | tf_op jit(solution)/shard_map/ppermute | solution.py:179
  11.8 1.9 %pack_blocks.1.b0 = bf16[576,128]{1,0:T(8,128)(2,1)} custom-call(bf16[13,13,8,36]{3,2,1,0:T(8,128)(2,1)} %bitcast.33), custom_call_target="tpu_custom_call" | custom-call | tf_op jit(solution)/shard_map/pack_blocks/pallas_call | solution.py:36
  13.7 1.9 %collective-permute-start.2 = (bf16[576,128]{1,0:T(8,128)(2,1)}, bf16[576,128]{1,0:T(8,128)(2,1)S(1)}, u32[]{:S(2)}, u32[]{:S(2)}) collective-permute-start(bf16[576,128]{1,0:T(8,128)(2,1)} %pack_blocks.1.b0), channel_id=1, source_target_pairs={{0,1},{1,2},{2,3},{3,0},{4,5},{5,6},{6,7},{7,4},{8,9},{9,10},{10,1... | collective-permute-start | bytes 442376 | tf_op jit(solution)/shard_map/ppermute | solution.py:193
  15.6 3.2 %collective-permute-start.1 = (bf16[576,128]{1,0:T(8,128)(2,1)}, bf16[576,128]{1,0:T(8,128)(2,1)S(1)}, u32[]{:S(2)}, u32[]{:S(2)}) collective-permute-start(bf16[576,128]{1,0:T(8,128)(2,1)} %pack_blocks.1.b0), channel_id=1, source_target_pairs={{0,2},{1,3},{2,0},{3,1},{4,6},{5,7},{6,4},{7,5},{8,10},{9,11},{10,... | collective-permute-start | bytes 442376 | tf_op jit(solution)/shard_map/ppermute | solution.py:193
  18.9 2.1 %collective-permute-start = (bf16[576,128]{1,0:T(8,128)(2,1)}, bf16[576,128]{1,0:T(8,128)(2,1)S(1)}, u32[]{:S(2)}, u32[]{:S(2)}) collective-permute-start(bf16[576,128]{1,0:T(8,128)(2,1)} %pack_blocks.1.b0), channel_id=1, source_target_pairs={{0,3},{1,0},{2,1},{3,2},{4,7},{5,4},{6,5},{7,6},{8,11},{9,8},{10,9... | collective-permute-start | bytes 442376 | tf_op jit(solution)/shard_map/ppermute | solution.py:193
  21.0 1.4 %copy.8.kv_ref = f32[8,2]{1,0:T(8,128)} copy(f32[8,2]{0,1:T(2,128)} %param.8) | data formatting | bytes 128 | tf_op args[2]
  22.3 1.3 %add_select_fusion.refs_0_ = s32[32,36]{1,0:T(8,128)} fusion(s32[36,32]{0,1:T(8,128)} %param.9, s32[]{:T(128)S(6)} %sub.10), kind=kLoop, calls=%fused_computation | loop fusion | flops 9216 | bytes 9220 | tf_op jit(solution)/shard_map/jit(remainder)/select_n | solution.py:198
  23.7 0.1 collective-permute-done.2.b3
  23.8 0.0 copy-start.4
  23.8 8.9 %collective-permute-done.1.b2 = bf16[576,128]{1,0:T(8,128)(2,1)S(1)} collective-permute-done((bf16[576,128]{1,0:T(8,128)(2,1)}, bf16[576,128]{1,0:T(8,128)(2,1)S(1)}, u32[]{:S(2)}, u32[]{:S(2)}) %collective-permute-start.1) | collective-permute-done | bytes 147488 | tf_op jit(solution)/shard_map/ppermute | solution.py:193
  32.7 0.0 copy-start.5
  32.7 0.0 collective-permute-done.b1
  32.7 0.0 copy-start.6
  32.7 0.0 copy-done.4
  32.7 0.6 copy-done.5
  33.3 0.1 copy-done.6
  33.4 3.8 %phase_blocks.1.refs_2_ = bf16[2304,512]{1,0:T(8,128)(2,1)} custom-call(f32[8,2]{1,0:T(8,128)} %copy.8.kv_ref, s32[1]{0:T(128)} %bitcast.1.spot_ref.refs_1_, s32[32,36]{1,0:T(8,128)} %bitcast.34, s32[1,36]{1,0:T(1,128)} %bitcast.35, bf16[576,128]{1,0:T(8,128)(2,1)} %pack_blocks.1.b0, bf16[576,128]{1,0:T(8,128)(2,1)} %copy-done.6, ...), custom_call_target="tpu_custom_call" | custom-call | tf_op jit(solution)/shard_map/phase_blocks/pallas_call | solution.py:86
  37.2 0.0 collective-permute-done.3.refs_4_
  37.2 0.0 copy-start
  37.2 0.0 collective-permute-done.4.refs_5_
  37.2 0.0 copy-start.1
  37.2 0.7 copy-done
  37.9 0.1 copy-done.1
  38.1 11.3 %apply_blocks.2 = (bf16[1872,128]{1,0:T(8,128)(2,1)}, bf16[1664,128]{1,0:T(8,128)(2,1)}, bf16[1664,128]{1,0:T(8,128)(2,1)}) custom-call(s32[32,36]{1,0:T(8,128)} %add_select_fusion.refs_0_, s32[1]{0:T(128)} %bitcast.1.spot_ref.refs_1_, bf16[2304,512]{1,0:T(8,128)(2,1)} %phase_blocks.1.refs_2_, bf16[1872,128]{1,0:T(8,128)(2,1)} %bitcast.28, ...), custom_call_target="tpu_custom_call" | custom-call | tf_op jit(solution)/shard_map/apply_blocks/pallas_call | solution.py:162
  49.4 12.3 %collective-permute-start.5 = (bf16[1664,128]{1,0:T(8,128)(2,1)}, bf16[1664,128]{1,0:T(8,128)(2,1)S(1)}, u32[]{:S(2)}, u32[]{:S(2)}) collective-permute-start(bf16[1664,128]{1,0:T(8,128)(2,1)} %get-tuple-element.6), channel_id=1, source_target_pairs={{0,4},{4,8},{8,12},{12,16},{16,20},{20,24},{24,28},{28,32},{32,36}... | collective-permute-start | bytes 1277960 | tf_op jit(solution)/shard_map/ppermute | solution.py:178
  61.7 1.9 %collective-permute-start.6 = (bf16[1664,128]{1,0:T(8,128)(2,1)}, bf16[1664,128]{1,0:T(8,128)(2,1)S(1)}, u32[]{:S(2)}, u32[]{:S(2)}) collective-permute-start(bf16[1664,128]{1,0:T(8,128)(2,1)} %get-tuple-element.7), channel_id=1, source_target_pairs={{4,0},{8,4},{12,8},{16,12},{20,16},{24,20},{28,24},{32,28},{36,32}... | collective-permute-start | bytes 1277960 | tf_op jit(solution)/shard_map/ppermute | solution.py:179
  63.6 6.9 %collective-permute-done.5.refs_4_ = bf16[1664,128]{1,0:T(8,128)(2,1)S(1)} collective-permute-done((bf16[1664,128]{1,0:T(8,128)(2,1)}, bf16[1664,128]{1,0:T(8,128)(2,1)S(1)}, u32[]{:S(2)}, u32[]{:S(2)}) %collective-permute-start.5) | collective-permute-done | bytes 426016 | tf_op jit(solution)/shard_map/ppermute | solution.py:178
  70.5 0.0 copy-start.2
  70.5 13.0 %collective-permute-done.6.refs_5_ = bf16[1664,128]{1,0:T(8,128)(2,1)S(1)} collective-permute-done((bf16[1664,128]{1,0:T(8,128)(2,1)}, bf16[1664,128]{1,0:T(8,128)(2,1)S(1)}, u32[]{:S(2)}, u32[]{:S(2)}) %collective-permute-start.6) | collective-permute-done | bytes 426016 | tf_op jit(solution)/shard_map/ppermute | solution.py:179
  83.6 0.0 copy-start.3
  83.6 0.0 copy-done.2
  83.6 0.8 copy-done.3
  84.3 11.0 %apply_blocks.3 = bf16[1872,128]{1,0:T(8,128)(2,1)} custom-call(s32[32,36]{1,0:T(8,128)} %add_select_fusion.refs_0_, s32[1]{0:T(128)} %bitcast.1.spot_ref.refs_1_, bf16[2304,512]{1,0:T(8,128)(2,1)} %phase_blocks.1.refs_2_, bf16[1872,128]{1,0:T(8,128)(2,1)} %get-tuple-element.5.refs_3_, bf16[1664,128]{1,0:T(8,128)(2,1)} %copy-done.2, bf16[1664,128]{1,0:T(8,128)(2,1)} %copy-done.3), custom_call_target="tpu_custom_call" | custom-call | tf_op jit(solution)/shard_map/apply_blocks/pallas_call | solution.py:162
Async XLA Ops:
  1.9 35.3 %collective-permute-start.3 = (bf16[1664,128]{1,0:T(8,128)(2,1)S(1)}, bf16[1664,128]{1,0:T(8,128)(2,1)S(1)}, u32[]{:S(2)}, u32[]{:S(2)}) collective-permute-start(bf16[1664,128]{1,0:T(8,128)(2,1)S(1)} %bitcast.32), channel_id=1, source_target_pairs={{0,4},{4,8},{8,12},{12,16},{16,20},{20,24},{24,28},{28,32},{32,36}... | collective-permute-start | bytes 1277960 | tf_op jit(solution)/shard_map/ppermute | solution.py:178
  9.9 27.3 %collective-permute-start.4 = (bf16[1664,128]{1,0:T(8,128)(2,1)S(1)}, bf16[1664,128]{1,0:T(8,128)(2,1)S(1)}, u32[]{:S(2)}, u32[]{:S(2)}) collective-permute-start(bf16[1664,128]{1,0:T(8,128)(2,1)S(1)} %bitcast.31), channel_id=1, source_target_pairs={{4,0},{8,4},{12,8},{16,12},{20,16},{24,20},{28,24},{32,28},{36,32}... | collective-permute-start | bytes 1277960 | tf_op jit(solution)/shard_map/ppermute | solution.py:179
  13.7 10.1 %collective-permute-start.2 = (bf16[576,128]{1,0:T(8,128)(2,1)}, bf16[576,128]{1,0:T(8,128)(2,1)S(1)}, u32[]{:S(2)}, u32[]{:S(2)}) collective-permute-start(bf16[576,128]{1,0:T(8,128)(2,1)} %pack_blocks.1.b0), channel_id=1, source_target_pairs={{0,1},{1,2},{2,3},{3,0},{4,5},{5,6},{6,7},{7,4},{8,9},{9,10},{10,1... | collective-permute-start | bytes 442376 | tf_op jit(solution)/shard_map/ppermute | solution.py:193
  15.6 17.0 %collective-permute-start.1 = (bf16[576,128]{1,0:T(8,128)(2,1)}, bf16[576,128]{1,0:T(8,128)(2,1)S(1)}, u32[]{:S(2)}, u32[]{:S(2)}) collective-permute-start(bf16[576,128]{1,0:T(8,128)(2,1)} %pack_blocks.1.b0), channel_id=1, source_target_pairs={{0,2},{1,3},{2,0},{3,1},{4,6},{5,7},{6,4},{7,5},{8,10},{9,11},{10,... | collective-permute-start | bytes 442376 | tf_op jit(solution)/shard_map/ppermute | solution.py:193
  18.9 13.8 %collective-permute-start = (bf16[576,128]{1,0:T(8,128)(2,1)}, bf16[576,128]{1,0:T(8,128)(2,1)S(1)}, u32[]{:S(2)}, u32[]{:S(2)}) collective-permute-start(bf16[576,128]{1,0:T(8,128)(2,1)} %pack_blocks.1.b0), channel_id=1, source_target_pairs={{0,3},{1,0},{2,1},{3,2},{4,7},{5,4},{6,5},{7,6},{8,11},{9,8},{10,9... | collective-permute-start | bytes 442376 | tf_op jit(solution)/shard_map/ppermute | solution.py:193
  23.8 8.9 %copy-start.4 = (bf16[576,128]{1,0:T(8,128)(2,1)}, bf16[576,128]{1,0:T(8,128)(2,1)S(1)}, u32[]{:S(2)}) copy-start(bf16[576,128]{1,0:T(8,128)(2,1)S(1)} %collective-permute-done.2.b3) | copy-start | bytes 442372
  32.7 0.7 copy-start.5
  32.7 0.7 copy-start.6
  37.2 0.8 copy-start
  37.2 0.9 copy-start.1
  49.4 21.1 %collective-permute-start.5 = (bf16[1664,128]{1,0:T(8,128)(2,1)}, bf16[1664,128]{1,0:T(8,128)(2,1)S(1)}, u32[]{:S(2)}, u32[]{:S(2)}) collective-permute-start(bf16[1664,128]{1,0:T(8,128)(2,1)} %get-tuple-element.6), channel_id=1, source_target_pairs={{0,4},{4,8},{8,12},{12,16},{16,20},{20,24},{24,28},{28,32},{32,36}... | collective-permute-start | bytes 1277960 | tf_op jit(solution)/shard_map/ppermute | solution.py:178
  61.7 21.9 %collective-permute-start.6 = (bf16[1664,128]{1,0:T(8,128)(2,1)}, bf16[1664,128]{1,0:T(8,128)(2,1)S(1)}, u32[]{:S(2)}, u32[]{:S(2)}) collective-permute-start(bf16[1664,128]{1,0:T(8,128)(2,1)} %get-tuple-element.7), channel_id=1, source_target_pairs={{4,0},{8,4},{12,8},{16,12},{20,16},{24,20},{28,24},{32,28},{36,32}... | collective-permute-start | bytes 1277960 | tf_op jit(solution)/shard_map/ppermute | solution.py:179
  70.5 13.0 %copy-start.2 = (bf16[1664,128]{1,0:T(8,128)(2,1)}, bf16[1664,128]{1,0:T(8,128)(2,1)S(1)}, u32[]{:S(2)}) copy-start(bf16[1664,128]{1,0:T(8,128)(2,1)S(1)} %collective-permute-done.5.refs_4_) | copy-start | bytes 1277956
  83.6 0.8 copy-start.3

commit v2 on v1

v2 whole, which is shorter than its diff:
```python
import math

import jax
import jax.numpy as jnp
from jax import lax
from jax.experimental import pallas as pl
from jax.experimental.pallas import tpu as pltpu
from jax.sharding import PartitionSpec as P

REACH = 32
NO = 13
NV = 128
SLOTS = 32
OWN = 8
LANES = 128
ROWS = 16
SPLIT = 4
UNROLL = 2
VMEM = pl.BlockSpec(memory_space=pltpu.VMEM)
SMEM = pl.BlockSpec(memory_space=pltpu.SMEM)


def pack_kernel(blocks_ref, out_ref, buf):
    atoms = blocks_ref.shape[3]
    r = lax.broadcasted_iota(jnp.int32, (NO * OWN, LANES), 0)
    c = lax.broadcasted_iota(jnp.int32, (NO * OWN, LANES), 1)
    place = ((r % OWN == c // ROWS) & (r // OWN == c % ROWS)).astype(jnp.float32).astype(jnp.bfloat16)
    for x in range(NO):
        b = blocks_ref[x].astype(jnp.float32).reshape(NO * OWN, atoms).astype(jnp.bfloat16)
        t = lax.dot_general(b, place, (((0,), (0,)), ((), ())), preferred_element_type=jnp.float32)
        buf[pl.ds(x, atoms, stride=NO), :] = t
    out_ref[...] = buf[...].astype(jnp.bfloat16)


def pack_blocks(blocks):
    atoms = blocks.shape[0]
    return pl.pallas_call(
        pack_kernel,
        out_shape=jax.ShapeDtypeStruct((atoms * NO, LANES), jnp.bfloat16),
        in_specs=[VMEM],
        out_specs=VMEM,
        scratch_shapes=[pltpu.VMEM((atoms * NO, LANES), jnp.float32)],
        name="pack_blocks",
    )(jnp.transpose(blocks, (2, 3, 1, 0)))


def phase_kernel(kv_ref, spot_ref, offs_ref, counts_ref, b0, b1, b2, b3, h_ref, ce, se, bf):
    atoms = offs_ref.shape[1]
    nk = h_ref.shape[0] // (atoms * 2 * ROWS)
    mine = spot_ref[0]
    offs = offs_ref[...]
    g0 = (offs // 7 - 3).astype(jnp.float32)
    g1 = (offs % 7 - 3).astype(jnp.float32)
    slot = lax.broadcasted_iota(jnp.int32, offs.shape, 0)
    live = slot < counts_ref[...]
    width = 4 * LANES
    r = lax.broadcasted_iota(jnp.int32, (SLOTS, width), 0)
    c = lax.broadcasted_iota(jnp.int32, (SLOTS, width), 1)
    group = (c // LANES) ^ mine
    spread = (r == group * OWN + (c % LANES) // ROWS).astype(jnp.float32)
    for k in range(nk):
        theta = (2.0 * math.pi) * (kv_ref[nk * mine + k, 0] * g0 + kv_ref[nk * mine + k, 1] * g1)
        for dst, val in ((ce, jnp.cos(theta)), (se, jnp.sin(theta))):
            wide = lax.dot_general(
                jnp.where(live, val, 0.0), spread, (((0,), (0,)), ((), ())),
                precision=lax.Precision.HIGHEST, preferred_element_type=jnp.float32)
            for g in range(4):
                top = (g * nk + k) * atoms
                dst[top:top + atoms, :] = wide[:, g * LANES:(g + 1) * LANES]
    pad = bf.shape[0] // 4
    for g, piece in enumerate((b0, b1, b2, b3)):
        bf[g * pad:g * pad + atoms * NO, :] = piece[...].astype(jnp.float32)

    def one(a, carry):
        for g in range(4):
            lanes = slice(g * LANES, (g + 1) * LANES)
            block = bf[pl.ds(g * pad + a * NO, ROWS), :]
            for k in range(nk):
                row = pl.multiple_of((a * nk + k) * 2 * ROWS, 2 * ROWS)
                h_ref[pl.ds(row, ROWS), lanes] = (ce[pl.ds((g * nk + k) * atoms + a, 1), :] * block).astype(jnp.bfloat16)
                h_ref[pl.ds(row + ROWS, ROWS), lanes] = (se[pl.ds((g * nk + k) * atoms + a, 1), :] * block).astype(jnp.bfloat16)
        return carry

    lax.fori_loop(0, atoms, one, 0)


def phase_blocks(kvecs, spot, offsets, counts, pieces, nk):
    atoms = offsets.shape[0]
    return pl.pallas_call(
        phase_kernel,
        out_shape=jax.ShapeDtypeStruct((nk * atoms * 2 * ROWS, 4 * LANES), jnp.bfloat16),
        in_specs=[SMEM, SMEM] + [VMEM] * 6,
        out_specs=VMEM,
        scratch_shapes=[pltpu.VMEM((4 * nk * atoms, LANES), jnp.float32)] * 2
        + [pltpu.VMEM((4 * (atoms * NO + 4), LANES), jnp.float32)],
        name="phase_blocks",
    )(kvecs, spot, offsets.T, counts.reshape(1, atoms), *pieces)


def apply_kernel(nbr_ref, spot_ref, h_ref, own_ref, a_ref, b_ref, *rest, halos):
    if halos:
        out_ref, send_a, send_b, flat, win, acc = rest
    else:
        out_ref, flat, win, acc = rest
    atoms = nbr_ref.shape[1]
    nk = h_ref.shape[0] // (atoms * 2 * ROWS)
    window = atoms + 2 * REACH
    edge = REACH * 2 * NO
    mid = atoms * 2 * NO
    span = edge * 2 + mid
    mine = spot_ref[0]
    odd = spot_ref[1]
    right = edge + mid
    for k in range(nk):
        to_a = pl.multiple_of(k * span + odd * right, 8)
        to_b = pl.multiple_of(k * span + (1 - odd) * right, 8)
        flat[pl.ds(to_a, edge), :] = a_ref[k * edge:(k + 1) * edge, :].astype(jnp.float32)
        flat[pl.ds(to_b, edge), :] = b_ref[k * edge:(k + 1) * edge, :].astype(jnp.float32)
        flat[k * span + edge:k * span + edge + mid, :] = own_ref[k * mid:(k + 1) * mid, :].astype(jnp.float32)
    flat[nk * span:, :] = jnp.zeros((flat.shape[0] - nk * span, NV), jnp.float32)

    def split(i, carry):
        for j in range(SPLIT):
            w = i * SPLIT + j
            for k in range(nk):
                for part in range(2):
                    rows = flat[pl.ds(k * span + w * 2 * NO + part, ROWS, stride=2), :]
                    win[w, k, part] = rows.astype(jnp.bfloat16)
        return carry

    lax.fori_loop(0, window // SPLIT, split, 0)

    def some(i, carry):
        for j in range(UNROLL):
            a = i * UNROLL + j
            spots = [nbr_ref[(mine ^ g) * OWN + s, a] for g in range(4) for s in range(OWN)]
            for k in range(nk):
                row = pl.multiple_of((a * nk + k) * 2 * ROWS, 2 * ROWS)
                total = None
                for half in range(2):
                    tiles = [jnp.concatenate([win[w, k, 0], win[w, k, 1]], axis=1)
                             for w in spots[half * 2 * OWN:(half + 1) * 2 * OWN]]
                    rhs = jnp.concatenate(tiles, axis=0)
                    lhs = h_ref[pl.ds(row, 2 * ROWS), 2 * half * LANES:(2 * half + 2) * LANES]
                    got = jnp.dot(lhs, rhs, preferred_element_type=jnp.float32)
                    total = got if total is None else total + got
                re = total[:ROWS, :NV] - total[ROWS:, NV:]
                im = total[:ROWS, NV:] + total[ROWS:, :NV]
                start = (k * atoms + a) * 2 * NO
                acc[pl.ds(start, NO, stride=2), :] = re[:NO]
                acc[pl.ds(start + 1, NO, stride=2), :] = im[:NO]
        return carry

    lax.fori_loop(0, atoms // UNROLL, some, 0)
    out_ref[...] = acc[...].astype(jnp.bfloat16)
    if halos:
        for k in range(nk):
            top = pl.multiple_of(k * mid + odd * (mid - edge), 8)
            send_a[k * edge:(k + 1) * edge, :] = acc[pl.ds(top, edge), :].astype(jnp.bfloat16)
            top = pl.multiple_of(k * mid + (1 - odd) * (mid - edge), 8)
            send_b[k * edge:(k + 1) * edge, :] = acc[pl.ds(top, edge), :].astype(jnp.bfloat16)


def apply_blocks(nbr, spot, h, own, from_a, from_b, halos):
    atoms = nbr.shape[1]
    nk = h.shape[0] // (atoms * 2 * ROWS)
    edge = nk * REACH * 2 * NO
    window = atoms + 2 * REACH
    shapes = [jax.ShapeDtypeStruct(own.shape, jnp.bfloat16)]
    if halos:
        shapes += [jax.ShapeDtypeStruct((edge, NV), jnp.bfloat16)] * 2
    return pl.pallas_call(
        lambda *refs: apply_kernel(*refs, halos=halos),
        out_shape=shapes,
        in_specs=[SMEM, SMEM] + [VMEM] * 4,
        out_specs=[VMEM] * len(shapes),
        scratch_shapes=[
            pltpu.VMEM((nk * window * 2 * NO + ROWS, NV), jnp.float32),
            pltpu.VMEM((window, nk, 2, ROWS, NV), jnp.bfloat16),
            pltpu.VMEM((own.shape[0], NV), jnp.float32),
        ],
        name="apply_blocks",
    )(nbr, spot, h, own, from_a, from_b)


def exchange(send_a, send_b):
    n = lax.axis_size("atoms")
    across = [(i, (i + 1) % n if i % 2 else (i - 1) % n) for i in range(n)]
    return (lax.ppermute(send_a, "atoms", across),
            lax.ppermute(send_b, "atoms", [(i, i ^ 1) for i in range(n)]))


def per_device(blocks, vectors, kvecs, neighbours, offsets, counts):
    atoms = blocks.shape[0]
    nk = vectors.shape[0]
    at = lax.axis_index("atoms").astype(jnp.int32)
    odd = at % 2
    rows = jnp.transpose(vectors, (0, 1, 3, 2, 4)).reshape(nk * atoms * NO * 2, NV)
    per_k = rows.reshape(nk, atoms * NO * 2, NV)
    edge = REACH * NO * 2
    rest = atoms * NO * 2 - edge
    packed = pack_blocks(blocks)
    owners = lax.axis_size("kpt")
    pieces = [packed] + [
        lax.ppermute(packed, "kpt", [(i, i ^ d) for i in range(owners)]) for d in range(1, owners)
    ]
    from_a, from_b = exchange(
        lax.dynamic_slice_in_dim(per_k, odd * rest, edge, 1).reshape(nk * edge, NV),
        lax.dynamic_slice_in_dim(per_k, (1 - odd) * rest, edge, 1).reshape(nk * edge, NV))
    spot = jnp.stack([lax.axis_index("kpt").astype(jnp.int32), odd])
    total_atoms = atoms * lax.axis_size("atoms")
    nbr = (neighbours.T - (at * atoms - REACH) + total_atoms) % total_atoms
    h = phase_blocks(kvecs, spot, offsets, counts, pieces, nk)
    first, send_a, send_b = apply_blocks(nbr, spot, h, rows, from_a, from_b, True)
    from_a, from_b = exchange(send_a, send_b)
    (second,) = apply_blocks(nbr, spot, h, first, from_a, from_b, False)

    def whole(flat):
        return jnp.transpose(flat.reshape(nk, atoms, NO, 2, NV), (0, 1, 3, 2, 4))

    return whole(first), whole(second)


def solution(mesh):
    placed = (
        P("atoms", "kpt", None, None),
        P("kpt", "atoms", None, None, None),
        P(),
        P("atoms", None),
        P("atoms", None),
        P("atoms"),
    )
    return jax.shard_map(
        per_device,
        mesh=mesh,
        in_specs=placed,
        out_specs=(P("kpt", "atoms", None, None, None), P("kpt", "atoms", None, None, None)),
        check_vma=False,
    )
```

time: 95.8 us -> 83 us (0.87)
  the two profiles are of different devices: /device:TPU:255 before, /device:TPU:24 now
where the time goes in v2:
time: 83 us; the launch traced here: 82.6 us
  starting transfers between devices  33.5 us (40%)
  Pallas kernels  22.9 us (28%)
  waiting for transfers between devices  18.4 us (22%)
  local copies, waits for them, and re-layouts  5.07 us (6%)
  other arithmetic  1.99 us (2%)
    ppermute x2, starting transfers between devices, exchange(): lax.ppermute(send_a, 'atoms', across)  19.5 us
    pallas_call x2, Pallas kernels, apply_blocks(): pl.pallas_call(lambda *refs: apply_kernel(*refs, halos=halos), out_shape=...  17.3 us
    ppermute x2, waiting for transfers between devices, exchange(): lax.ppermute(send_a, 'atoms', across)  15 us
    ppermute x3, starting transfers between devices, per_device(): lax.ppermute(packed, 'kpt', [(i, i ^ d) for i in range(owners)])  10.1 us
    ppermute x2, starting transfers between devices, exchange(): lax.ppermute(send_b, 'atoms', [(i, i ^ 1) for i in range(n)])  3.84 us
    unnamed x15, local copies, waits for them, and re-layouts  3.77 us
    pallas_call x1, Pallas kernels, phase_blocks(): pl.pallas_call(phase_kernel, out_shape=jax.ShapeDtypeStruct((nk * atoms *...  3.68 us
    ppermute x3, waiting for transfers between devices, per_device(): lax.ppermute(packed, 'kpt', [(i, i ^ d) for i in range(owners)])  3.38 us
  transfers between devices with their start and end apart: 7, of which 3 were waited for; matrix products, arithmetic and copies ran while one was open for 4% of the time, Pallas kernels for 7%

profile of v2, /device:TPU:24, one launch (start us, length us, event | category | flops | bytes accessed | tf_op | source)
XLA Modules:
  0.0 82.6 jit_solution(12372273148612894289)
XLA Ops:
  0.7 1.3 %constant_dynamic-slice_fusion = (bf16[2,832,128]{2,1,0:T(8,128)(2,1)S(1)}, bf16[2,832,128]{2,1,0:T(8,128)(2,1)S(1)}) fusion(bf16[2,936,128]{2,1,0:T(8,128)(2,1)} %bitcast.28, s32[]{:T(128)S(6)} %select_n.22, s32[]{:T(128)S(6)} %select_n.21), kind=kLoop, calls=%fused_computation.6 | loop fusion | bytes 1703944 | tf_op jit(solution)/shard_map/dynamic_slice | solution.py:209
  2.0 15.1 %collective-permute-start.3 = (bf16[1664,128]{1,0:T(8,128)(2,1)S(1)}, bf16[1664,128]{1,0:T(8,128)(2,1)S(1)}, u32[]{:S(2)}, u32[]{:S(2)}) collective-permute-start(bf16[1664,128]{1,0:T(8,128)(2,1)S(1)} %bitcast.33), channel_id=1, source_target_pairs={{0,508},{4,8},{8,4},{12,16},{16,12},{20,24},{24,20},{28,32},{32,28... | collective-permute-start | bytes 1277960 | tf_op jit(solution)/shard_map/ppermute | solution.py:189
  17.1 1.9 %collective-permute-start.4 = (bf16[1664,128]{1,0:T(8,128)(2,1)S(1)}, bf16[1664,128]{1,0:T(8,128)(2,1)S(1)}, u32[]{:S(2)}, u32[]{:S(2)}) collective-permute-start(bf16[1664,128]{1,0:T(8,128)(2,1)S(1)} %bitcast.32), channel_id=1, source_target_pairs={{0,4},{4,0},{8,12},{12,8},{16,20},{20,16},{24,28},{28,24},{32,36},... | collective-permute-start | bytes 1277960 | tf_op jit(solution)/shard_map/ppermute | solution.py:190
  19.0 1.9 %pack_blocks.1.b0 = bf16[468,128]{1,0:T(8,128)(2,1)} custom-call(bf16[13,13,8,36]{3,2,1,0:T(8,128)(2,1)} %bitcast.34), custom_call_target="tpu_custom_call" | custom-call | tf_op jit(solution)/shard_map/pack_blocks/pallas_call | solution.py:37
  21.0 4.8 %collective-permute-start.2 = (bf16[468,128]{1,0:T(8,128)(2,1)}, bf16[468,128]{1,0:T(8,128)(2,1)S(1)}, u32[]{:S(2)}, u32[]{:S(2)}) collective-permute-start(bf16[468,128]{1,0:T(8,128)(2,1)} %pack_blocks.1.b0), channel_id=1, source_target_pairs={{0,3},{1,2},{2,1},{3,0},{4,7},{5,6},{6,5},{7,4},{8,11},{9,10},{10,... | collective-permute-start | bytes 359432 | tf_op jit(solution)/shard_map/ppermute | solution.py:205
  25.8 1.9 %collective-permute-start.1 = (bf16[468,128]{1,0:T(8,128)(2,1)}, bf16[468,128]{1,0:T(8,128)(2,1)S(1)}, u32[]{:S(2)}, u32[]{:S(2)}) collective-permute-start(bf16[468,128]{1,0:T(8,128)(2,1)} %pack_blocks.1.b0), channel_id=1, source_target_pairs={{0,2},{1,3},{2,0},{3,1},{4,6},{5,7},{6,4},{7,5},{8,10},{9,11},{10,... | collective-permute-start | bytes 359432 | tf_op jit(solution)/shard_map/ppermute | solution.py:205
  27.7 3.4 %collective-permute-start = (bf16[468,128]{1,0:T(8,128)(2,1)}, bf16[468,128]{1,0:T(8,128)(2,1)S(1)}, u32[]{:S(2)}, u32[]{:S(2)}) collective-permute-start(bf16[468,128]{1,0:T(8,128)(2,1)} %pack_blocks.1.b0), channel_id=1, source_target_pairs={{0,1},{1,0},{2,3},{3,2},{4,5},{5,4},{6,7},{7,6},{8,9},{9,8},{10,11... | collective-permute-start | bytes 359432 | tf_op jit(solution)/shard_map/ppermute | solution.py:205
  31.1 1.3 %add_select_fusion.refs_0_ = s32[32,36]{1,0:T(8,128)} fusion(s32[36,32]{0,1:T(8,128)} %param.9, s32[]{:T(128)S(6)} %sub.13), kind=kLoop, calls=%fused_computation | loop fusion | flops 9216 | bytes 9220 | tf_op jit(solution)/shard_map/jit(remainder)/select_n | solution.py:212
  32.4 1.3 %copy.8.kv_ref = f32[8,2]{1,0:T(8,128)} copy(f32[8,2]{0,1:T(2,128)} %param.8) | data formatting | bytes 128 | tf_op args[2]
  33.8 0.7 pad_add_fusion.spot_ref.refs_1_
  34.4 0.0 collective-permute-done.2.b3
  34.4 0.0 copy-start.4
  34.4 3.0 %collective-permute-done.1.b2 = bf16[468,128]{1,0:T(8,128)(2,1)S(1)} collective-permute-done((bf16[468,128]{1,0:T(8,128)(2,1)}, bf16[468,128]{1,0:T(8,128)(2,1)S(1)}, u32[]{:S(2)}, u32[]{:S(2)}) %collective-permute-start.1) | collective-permute-done | bytes 119840 | tf_op jit(solution)/shard_map/ppermute | solution.py:205
  37.4 0.0 copy-start.5
  37.4 0.4 collective-permute-done.b1
  37.8 0.0 copy-start.6
  37.8 0.0 copy-done.4
  37.8 0.2 copy-done.5
  38.0 0.4 copy-done.6
  38.5 3.7 %phase_blocks.1.refs_2_ = bf16[2304,512]{1,0:T(8,128)(2,1)} custom-call(f32[8,2]{1,0:T(8,128)} %copy.8.kv_ref, s32[2]{0:T(128)} %pad_add_fusion.spot_ref.refs_1_, s32[32,36]{1,0:T(8,128)} %bitcast.35, s32[1,36]{1,0:T(1,128)} %bitcast.36, bf16[468,128]{1,0:T(8,128)(2,1)} %pack_blocks.1.b0, bf16[468,128]{1,0:T(8,128)(2,1)} %copy-done.6, ...), custom_call_target="tpu_custom_call" | custom-call | tf_op jit(solution)/shard_map/phase_blocks/pallas_call | solution.py:89
  42.1 0.0 collective-permute-done.3.refs_4_
  42.1 0.0 copy-start
  42.1 0.0 collective-permute-done.4.refs_5_
  42.2 0.0 copy-start.1
  42.2 0.7 copy-done
  42.9 0.1 copy-done.1
  43.0 8.8 %apply_blocks.2 = (bf16[1872,128]{1,0:T(8,128)(2,1)}, bf16[1664,128]{1,0:T(8,128)(2,1)}, bf16[1664,128]{1,0:T(8,128)(2,1)}) custom-call(s32[32,36]{1,0:T(8,128)} %add_select_fusion.refs_0_, s32[2]{0:T(128)} %pad_add_fusion.spot_ref.refs_1_, bf16[2304,512]{1,0:T(8,128)(2,1)} %phase_blocks.1.refs_2_, bf16[1872,128]{1,0:T(8,128)(2,1)} %bitcast.29, ...), custom_call_target="tpu_custom_call" | custom-call | tf_op jit(solution)/shard_map/apply_blocks/pallas_call | solution.py:172
  51.8 4.4 %collective-permute-start.5 = (bf16[1664,128]{1,0:T(8,128)(2,1)}, bf16[1664,128]{1,0:T(8,128)(2,1)S(1)}, u32[]{:S(2)}, u32[]{:S(2)}) collective-permute-start(bf16[1664,128]{1,0:T(8,128)(2,1)} %get-tuple-element.6), channel_id=1, source_target_pairs={{0,508},{4,8},{8,4},{12,16},{16,12},{20,24},{24,20},{28,32},{32,28... | collective-permute-start | bytes 1277960 | tf_op jit(solution)/shard_map/ppermute | solution.py:189
  56.2 1.9 %collective-permute-start.6 = (bf16[1664,128]{1,0:T(8,128)(2,1)}, bf16[1664,128]{1,0:T(8,128)(2,1)S(1)}, u32[]{:S(2)}, u32[]{:S(2)}) collective-permute-start(bf16[1664,128]{1,0:T(8,128)(2,1)} %get-tuple-element.7), channel_id=1, source_target_pairs={{0,4},{4,0},{8,12},{12,8},{16,20},{20,16},{24,28},{28,24},{32,36},... | collective-permute-start | bytes 1277960 | tf_op jit(solution)/shard_map/ppermute | solution.py:190
  58.1 15.0 %collective-permute-done.5.refs_4_ = bf16[1664,128]{1,0:T(8,128)(2,1)S(1)} collective-permute-done((bf16[1664,128]{1,0:T(8,128)(2,1)}, bf16[1664,128]{1,0:T(8,128)(2,1)S(1)}, u32[]{:S(2)}, u32[]{:S(2)}) %collective-permute-start.5) | collective-permute-done | bytes 426016 | tf_op jit(solution)/shard_map/ppermute | solution.py:189
  73.1 0.0 copy-start.2
  73.2 0.0 collective-permute-done.6.refs_5_
  73.2 0.0 copy-start.3
  73.2 0.8 copy-done.2
  73.9 0.1 copy-done.3
  74.1 8.5 %apply_blocks.3 = bf16[1872,128]{1,0:T(8,128)(2,1)} custom-call(s32[32,36]{1,0:T(8,128)} %add_select_fusion.refs_0_, s32[2]{0:T(128)} %pad_add_fusion.spot_ref.refs_1_, bf16[2304,512]{1,0:T(8,128)(2,1)} %phase_blocks.1.refs_2_, bf16[1872,128]{1,0:T(8,128)(2,1)} %get-tuple-element.5.refs_3_, bf16[1664,128]{1,0:T(8,128)(2,1)} %copy-done.2, ...), custom_call_target="tpu_custom_call" | custom-call | tf_op jit(solution)/shard_map/apply_blocks/pallas_call | solution.py:172
Async XLA Ops:
  2.0 40.2 %collective-permute-start.3 = (bf16[1664,128]{1,0:T(8,128)(2,1)S(1)}, bf16[1664,128]{1,0:T(8,128)(2,1)S(1)}, u32[]{:S(2)}, u32[]{:S(2)}) collective-permute-start(bf16[1664,128]{1,0:T(8,128)(2,1)S(1)} %bitcast.33), channel_id=1, source_target_pairs={{0,508},{4,8},{8,4},{12,16},{16,12},{20,24},{24,20},{28,32},{32,28... | collective-permute-start | bytes 1277960 | tf_op jit(solution)/shard_map/ppermute | solution.py:189
  17.1 25.0 %collective-permute-start.4 = (bf16[1664,128]{1,0:T(8,128)(2,1)S(1)}, bf16[1664,128]{1,0:T(8,128)(2,1)S(1)}, u32[]{:S(2)}, u32[]{:S(2)}) collective-permute-start(bf16[1664,128]{1,0:T(8,128)(2,1)S(1)} %bitcast.32), channel_id=1, source_target_pairs={{0,4},{4,0},{8,12},{12,8},{16,20},{20,16},{24,28},{28,24},{32,36},... | collective-permute-start | bytes 1277960 | tf_op jit(solution)/shard_map/ppermute | solution.py:190
  21.0 13.5 %collective-permute-start.2 = (bf16[468,128]{1,0:T(8,128)(2,1)}, bf16[468,128]{1,0:T(8,128)(2,1)S(1)}, u32[]{:S(2)}, u32[]{:S(2)}) collective-permute-start(bf16[468,128]{1,0:T(8,128)(2,1)} %pack_blocks.1.b0), channel_id=1, source_target_pairs={{0,3},{1,2},{2,1},{3,0},{4,7},{5,6},{6,5},{7,4},{8,11},{9,10},{10,... | collective-permute-start | bytes 359432 | tf_op jit(solution)/shard_map/ppermute | solution.py:205
  25.8 11.6 %collective-permute-start.1 = (bf16[468,128]{1,0:T(8,128)(2,1)}, bf16[468,128]{1,0:T(8,128)(2,1)S(1)}, u32[]{:S(2)}, u32[]{:S(2)}) collective-permute-start(bf16[468,128]{1,0:T(8,128)(2,1)} %pack_blocks.1.b0), channel_id=1, source_target_pairs={{0,2},{1,3},{2,0},{3,1},{4,6},{5,7},{6,4},{7,5},{8,10},{9,11},{10,... | collective-permute-start | bytes 359432 | tf_op jit(solution)/shard_map/ppermute | solution.py:205
  27.7 10.1 %collective-permute-start = (bf16[468,128]{1,0:T(8,128)(2,1)}, bf16[468,128]{1,0:T(8,128)(2,1)S(1)}, u32[]{:S(2)}, u32[]{:S(2)}) collective-permute-start(bf16[468,128]{1,0:T(8,128)(2,1)} %pack_blocks.1.b0), channel_id=1, source_target_pairs={{0,1},{1,0},{2,3},{3,2},{4,5},{5,4},{6,7},{7,6},{8,9},{9,8},{10,11... | collective-permute-start | bytes 359432 | tf_op jit(solution)/shard_map/ppermute | solution.py:205
  34.4 3.4 %copy-start.4 = (bf16[468,128]{1,0:T(8,128)(2,1)}, bf16[468,128]{1,0:T(8,128)(2,1)S(1)}, u32[]{:S(2)}) copy-start(bf16[468,128]{1,0:T(8,128)(2,1)S(1)} %collective-permute-done.2.b3) | copy-start | bytes 359428
  37.4 0.6 copy-start.5
  37.8 0.6 copy-start.6
  42.1 0.8 copy-start
  42.2 0.9 %copy-start.1 = (bf16[1664,128]{1,0:T(8,128)(2,1)}, bf16[1664,128]{1,0:T(8,128)(2,1)S(1)}, u32[]{:S(2)}) copy-start(bf16[1664,128]{1,0:T(8,128)(2,1)S(1)} %collective-permute-done.4.refs_5_) | copy-start | bytes 1277956
  51.8 21.3 %collective-permute-start.5 = (bf16[1664,128]{1,0:T(8,128)(2,1)}, bf16[1664,128]{1,0:T(8,128)(2,1)S(1)}, u32[]{:S(2)}, u32[]{:S(2)}) collective-permute-start(bf16[1664,128]{1,0:T(8,128)(2,1)} %get-tuple-element.6), channel_id=1, source_target_pairs={{0,508},{4,8},{8,4},{12,16},{16,12},{20,24},{24,20},{28,32},{32,28... | collective-permute-start | bytes 1277960 | tf_op jit(solution)/shard_map/ppermute | solution.py:189
  56.2 16.9 %collective-permute-start.6 = (bf16[1664,128]{1,0:T(8,128)(2,1)}, bf16[1664,128]{1,0:T(8,128)(2,1)S(1)}, u32[]{:S(2)}, u32[]{:S(2)}) collective-permute-start(bf16[1664,128]{1,0:T(8,128)(2,1)} %get-tuple-element.7), channel_id=1, source_target_pairs={{0,4},{4,0},{8,12},{12,8},{16,20},{20,16},{24,28},{28,24},{32,36},... | collective-permute-start | bytes 1277960 | tf_op jit(solution)/shard_map/ppermute | solution.py:190
  73.1 0.8 copy-start.2
  73.2 0.9 %copy-start.3 = (bf16[1664,128]{1,0:T(8,128)(2,1)}, bf16[1664,128]{1,0:T(8,128)(2,1)S(1)}, u32[]{:S(2)}) copy-start(bf16[1664,128]{1,0:T(8,128)(2,1)S(1)} %collective-permute-done.6.refs_5_) | copy-start | bytes 1277956

commit v3 on v2

--- a/solution.py
+++ b/solution.py
@@ -7,17 +7,22 @@
 from jax.experimental.pallas import tpu as pltpu
 from jax.sharding import PartitionSpec as P
 
+
 REACH = 32
 NO = 13
 NV = 128
-SLOTS = 32
 OWN = 8
 LANES = 128
 ROWS = 16
 SPLIT = 4
-UNROLL = 2
+UNROLL = 4
 VMEM = pl.BlockSpec(memory_space=pltpu.VMEM)
 SMEM = pl.BlockSpec(memory_space=pltpu.SMEM)
+PARAMS = pltpu.CompilerParams(vmem_limit_bytes=24 << 20)
+
+
+def near(array):
+    return pltpu.with_memory_space_constraint(array, pltpu.VMEM)
 
 
 def pack_kernel(blocks_ref, out_ref, buf):
@@ -36,30 +41,36 @@
     atoms = blocks.shape[0]
     return pl.pallas_call(
         pack_kernel,
-        out_shape=jax.ShapeDtypeStruct((atoms * NO, LANES), jnp.bfloat16),
+        out_shape=pltpu.VMEM((atoms * NO, LANES), jnp.bfloat16),
         in_specs=[VMEM],
         out_specs=VMEM,
         scratch_shapes=[pltpu.VMEM((atoms * NO, LANES), jnp.float32)],
         name="pack_blocks",
+        compiler_params=PARAMS,
     )(jnp.transpose(blocks, (2, 3, 1, 0)))
 
 
-def phase_kernel(kv_ref, spot_ref, offs_ref, counts_ref, b0, b1, b2, b3, h_ref, ce, se, bf):
-    atoms = offs_ref.shape[1]
-    nk = h_ref.shape[0] // (atoms * 2 * ROWS)
-    mine = spot_ref[0]
+def trig_kernel(kv_ref, nbr_ref, offs_ref, counts_ref, ce, se, local_ref):
+    slots, atoms = offs_ref.shape
+    nk = ce.shape[0] // (4 * atoms)
+    mine = lax.axis_index("kpt")
+    at = lax.axis_index("atoms")
+    total = atoms * lax.axis_size("atoms")
+    place = nbr_ref[...] - (at * atoms - REACH)
+    place = jnp.where(place < 0, place + total, place)
+    local_ref[...] = jnp.where(place >= total, place - total, place)
     offs = offs_ref[...]
     g0 = (offs // 7 - 3).astype(jnp.float32)
     g1 = (offs % 7 - 3).astype(jnp.float32)
     slot = lax.broadcasted_iota(jnp.int32, offs.shape, 0)
     live = slot < counts_ref[...]
     width = 4 * LANES
-    r = lax.broadcasted_iota(jnp.int32, (SLOTS, width), 0)
-    c = lax.broadcasted_iota(jnp.int32, (SLOTS, width), 1)
+    r = lax.broadcasted_iota(jnp.int32, (slots, width), 0)
+    c = lax.broadcasted_iota(jnp.int32, (slots, width), 1)
     group = (c // LANES) ^ mine
     spread = (r == group * OWN + (c % LANES) // ROWS).astype(jnp.float32)
     for k in range(nk):
-        theta = (2.0 * math.pi) * (kv_ref[nk * mine + k, 0] * g0 + kv_ref[nk * mine + k, 1] * g1)
+        theta = (2.0 * math.pi) * (kv_ref[0, nk * mine + k] * g0 + kv_ref[1, nk * mine + k] * g1)
         for dst, val in ((ce, jnp.cos(theta)), (se, jnp.sin(theta))):
             wide = lax.dot_general(
                 jnp.where(live, val, 0.0), spread, (((0,), (0,)), ((), ())),
@@ -67,37 +78,57 @@
             for g in range(4):
                 top = (g * nk + k) * atoms
                 dst[top:top + atoms, :] = wide[:, g * LANES:(g + 1) * LANES]
+
+
+def trig(kvecs, neighbours, offsets, counts, nk):
+    atoms, slots = offsets.shape
+    wide = pltpu.VMEM((4 * nk * atoms, LANES), jnp.float32)
+    return pl.pallas_call(
+        trig_kernel,
+        out_shape=[wide, wide, jax.ShapeDtypeStruct((slots, atoms), jnp.int32)],
+        in_specs=[SMEM] + [VMEM] * 3,
+        out_specs=[VMEM] * 3,
+        name="trig",
+        compiler_params=PARAMS,
+    )(kvecs.T, neighbours.T, offsets.T, counts.reshape(1, atoms))
+
+
+def phase_kernel(ce, se, b0, b1, b2, b3, h_ref, bf):
+    atoms = b0.shape[0] // NO
+    nk = h_ref.shape[0] // (atoms * 2 * ROWS)
     pad = bf.shape[0] // 4
     for g, piece in enumerate((b0, b1, b2, b3)):
         bf[g * pad:g * pad + atoms * NO, :] = piece[...].astype(jnp.float32)
 
-    def one(a, carry):
-        for g in range(4):
-            lanes = slice(g * LANES, (g + 1) * LANES)
-            block = bf[pl.ds(g * pad + a * NO, ROWS), :]
-            for k in range(nk):
-                row = pl.multiple_of((a * nk + k) * 2 * ROWS, 2 * ROWS)
-                h_ref[pl.ds(row, ROWS), lanes] = (ce[pl.ds((g * nk + k) * atoms + a, 1), :] * block).astype(jnp.bfloat16)
-                h_ref[pl.ds(row + ROWS, ROWS), lanes] = (se[pl.ds((g * nk + k) * atoms + a, 1), :] * block).astype(jnp.bfloat16)
+    def some(i, carry):
+        for j in range(2):
+            a = i * 2 + j
+            for g in range(4):
+                lanes = slice(g * LANES, (g + 1) * LANES)
+                block = bf[pl.ds(g * pad + a * NO, ROWS), :]
+                for k in range(nk):
+                    row = pl.multiple_of((a * nk + k) * 2 * ROWS, 2 * ROWS)
+                    top = (g * nk + k) * atoms + a
+                    h_ref[pl.ds(row, ROWS), lanes] = (ce[pl.ds(top, 1), :] * block).astype(jnp.bfloat16)
+                    h_ref[pl.ds(row + ROWS, ROWS), lanes] = (se[pl.ds(top, 1), :] * block).astype(jnp.bfloat16)
         return carry
 
-    lax.fori_loop(0, atoms, one, 0)
-
-
-def phase_blocks(kvecs, spot, offsets, counts, pieces, nk):
-    atoms = offsets.shape[0]
+    lax.fori_loop(0, atoms // 2, some, 0)
+
+
+def phase_blocks(ce, se, pieces, atoms, nk):
     return pl.pallas_call(
         phase_kernel,
-        out_shape=jax.ShapeDtypeStruct((nk * atoms * 2 * ROWS, 4 * LANES), jnp.bfloat16),
-        in_specs=[SMEM, SMEM] + [VMEM] * 6,
+        out_shape=pltpu.VMEM((nk * atoms * 2 * ROWS, 4 * LANES), jnp.bfloat16),
+        in_specs=[VMEM] * 6,
         out_specs=VMEM,
-        scratch_shapes=[pltpu.VMEM((4 * nk * atoms, LANES), jnp.float32)] * 2
-        + [pltpu.VMEM((4 * (atoms * NO + 4), LANES), jnp.float32)],
+        scratch_shapes=[pltpu.VMEM((4 * (atoms * NO + 4), LANES), jnp.float32)],
         name="phase_blocks",
-    )(kvecs, spot, offsets.T, counts.reshape(1, atoms), *pieces)
-
-
-def apply_kernel(nbr_ref, spot_ref, h_ref, own_ref, a_ref, b_ref, *rest, halos):
+        compiler_params=PARAMS,
+    )(near(ce), near(se), *[near(p) for p in pieces])
+
+
+def apply_kernel(nbr_ref, h_ref, own_ref, a_ref, b_ref, *rest, halos):
     if halos:
         out_ref, send_a, send_b, flat, win, acc = rest
     else:
@@ -108,8 +139,8 @@
     edge = REACH * 2 * NO
     mid = atoms * 2 * NO
     span = edge * 2 + mid
-    mine = spot_ref[0]
-    odd = spot_ref[1]
+    mine = lax.axis_index("kpt")
+    odd = lax.axis_index("atoms") % 2
     right = edge + mid
     for k in range(nk):
         to_a = pl.multiple_of(k * span + odd * right, 8)
@@ -161,18 +192,18 @@
             send_b[k * edge:(k + 1) * edge, :] = acc[pl.ds(top, edge), :].astype(jnp.bfloat16)
 
 
-def apply_blocks(nbr, spot, h, own, from_a, from_b, halos):
+def apply_blocks(nbr, h, own, from_a, from_b, halos):
     atoms = nbr.shape[1]
     nk = h.shape[0] // (atoms * 2 * ROWS)
     edge = nk * REACH * 2 * NO
     window = atoms + 2 * REACH
     shapes = [jax.ShapeDtypeStruct(own.shape, jnp.bfloat16)]
     if halos:
-        shapes += [jax.ShapeDtypeStruct((edge, NV), jnp.bfloat16)] * 2
+        shapes = [pltpu.VMEM(own.shape, jnp.bfloat16)] + [pltpu.VMEM((edge, NV), jnp.bfloat16)] * 2
     return pl.pallas_call(
         lambda *refs: apply_kernel(*refs, halos=halos),
         out_shape=shapes,
-        in_specs=[SMEM, SMEM] + [VMEM] * 4,
+        in_specs=[SMEM] + [VMEM] * 4,
         out_specs=[VMEM] * len(shapes),
         scratch_shapes=[
             pltpu.VMEM((nk * window * 2 * NO + ROWS, NV), jnp.float32),
@@ -180,17 +211,19 @@
             pltpu.VMEM((own.shape[0], NV), jnp.float32),
         ],
         name="apply_blocks",
-    )(nbr, spot, h, own, from_a, from_b)
+        compiler_params=PARAMS,
+    )(nbr, near(h), own, near(from_a), near(from_b))
 
 
 def exchange(send_a, send_b):
     n = lax.axis_size("atoms")
     across = [(i, (i + 1) % n if i % 2 else (i - 1) % n) for i in range(n)]
-    return (lax.ppermute(send_a, "atoms", across),
-            lax.ppermute(send_b, "atoms", [(i, i ^ 1) for i in range(n)]))
-
-
-def per_device(blocks, vectors, kvecs, neighbours, offsets, counts):
+    from_a = lax.ppermute(send_a, "atoms", across)
+    from_b = lax.ppermute(send_b, "atoms", [(i, i ^ 1) for i in range(n)])
+    return from_a, from_b
+
+
+def whole_step(blocks, vectors, kvecs, neighbours, offsets, counts):
     atoms = blocks.shape[0]
     nk = vectors.shape[0]
     at = lax.axis_index("atoms").astype(jnp.int32)
@@ -200,6 +233,7 @@
     edge = REACH * NO * 2
     rest = atoms * NO * 2 - edge
     packed = pack_blocks(blocks)
+    per_k, packed = lax.optimization_barrier((per_k, packed))
     owners = lax.axis_size("kpt")
     pieces = [packed] + [
         lax.ppermute(packed, "kpt", [(i, i ^ d) for i in range(owners)]) for d in range(1, owners)
@@ -207,13 +241,11 @@
     from_a, from_b = exchange(
         lax.dynamic_slice_in_dim(per_k, odd * rest, edge, 1).reshape(nk * edge, NV),
         lax.dynamic_slice_in_dim(per_k, (1 - odd) * rest, edge, 1).reshape(nk * edge, NV))
-    spot = jnp.stack([lax.axis_index("kpt").astype(jnp.int32), odd])
-    total_atoms = atoms * lax.axis_size("atoms")
-    nbr = (neighbours.T - (at * atoms - REACH) + total_atoms) % total_atoms
-    h = phase_blocks(kvecs, spot, offsets, counts, pieces, nk)
-    first, send_a, send_b = apply_blocks(nbr, spot, h, rows, from_a, from_b, True)
+    ce, se, nbr = trig(kvecs, neighbours, offsets, counts, nk)
+    h = phase_blocks(ce, se, pieces, atoms, nk)
+    first, send_a, send_b = apply_blocks(nbr, h, rows, from_a, from_b, True)
     from_a, from_b = exchange(send_a, send_b)
-    (second,) = apply_blocks(nbr, spot, h, first, from_a, from_b, False)
+    (second,) = apply_blocks(nbr, h, first, from_a, from_b, False)
 
     def whole(flat):
         return jnp.transpose(flat.reshape(nk, atoms, NO, 2, NV), (0, 1, 3, 2, 4))
@@ -231,7 +263,7 @@
         P("atoms"),
     )
     return jax.shard_map(
-        per_device,
+        whole_step,
         mesh=mesh,
         in_specs=placed,
         out_specs=(P("kpt", "atoms", None, None, None), P("kpt", "atoms", None, None, None)),

time: 83 us -> 72.8 us (0.88)
  Pallas kernels: 22.9 us -> 13.9 us
  other arithmetic: 1.99 us -> 0 us
    pallas_call x2, Pallas kernels: 17.3 us -> 12 us  [apply_blocks(): pl.pallas_call(lambda *refs: apply_kernel(*refs, halos=halos), out_shape=...]
    pallas_call x2 -> x3, Pallas kernels: 5.6 us -> 1.94 us  [the longest x1 1.11 us: trig(): pl.pallas_call(trig_kernel, out_shape=[wide, wide, jax.ShapeDtypeStruct((...]
    select_n x1 -> x0, other arithmetic: 1.33 us -> none  [per_device(): nbr = (neighbours.T - (at * atoms - REACH) + total_atoms) % total_atoms]
    unnamed x15 -> x13, local copies, waits for them, and re-layouts: 3.77 us -> 4.52 us
  transfers between devices with their start and end apart: 7 -> 7, of which waited for: 3 -> 2; matrix products, arithmetic and copies ran while one was open for 4% -> 1% of each run, Pallas kernels for 7% -> 2%
where the time goes in v3:
time: 72.8 us; the launch traced here: 72.3 us
  starting transfers between devices  33 us (45%)
  waiting for transfers between devices  18.8 us (26%)
  Pallas kernels  13.9 us (19%)
  local copies, waits for them, and re-layouts  5.77 us (8%)
  between operations  0.8 us (1%)
    ppermute x2, starting transfers between devices, exchange(): from_a = lax.ppermute(send_a, 'atoms', across)  19 us
    ppermute x2, waiting for transfers between devices, exchange(): from_a = lax.ppermute(send_a, 'atoms', across)  13.4 us
    pallas_call x2, Pallas kernels, apply_blocks(): pl.pallas_call(lambda *refs: apply_kernel(*refs, halos=halos), out_shape=...  12 us
    ppermute x3, starting transfers between devices, whole_step(): lax.ppermute(packed, 'kpt', [(i, i ^ d) for i in range(owners)])  10.1 us
    ppermute x3, waiting for transfers between devices, whole_step(): lax.ppermute(packed, 'kpt', [(i, i ^ d) for i in range(owners)])  5.45 us
    unnamed x13, local copies, waits for them, and re-layouts  4.52 us
    ppermute x2, starting transfers between devices, exchange(): from_b = lax.ppermute(send_b, 'atoms', [(i, i ^ 1) for i in range(n)])  3.84 us
  transfers between devices with their start and end apart: 7, of which 2 were waited for; matrix products, arithmetic and copies ran while one was open for 1% of the time, Pallas kernels for 2%

profile of v3, /device:TPU:24, one launch (start us, length us, event | category | flops | bytes accessed | tf_op | source)
XLA Modules:
  0.0 72.3 jit_solution(13485811180248889330)
XLA Ops:
  0.6 0.0 copy-start.1
  0.7 1.0 %copy-done.1 = bf16[36,8,13,13]{0,1,3,2:T(8,128)(2,1)S(1)} copy-done((bf16[36,8,13,13]{0,1,3,2:T(8,128)(2,1)S(1)}, bf16[36,8,13,13]{0,1,3,2:T(8,128)(2,1)}, u32[]{:S(2)}) %copy-start.1) | copy-done | bytes 97368
  1.6 0.3 pack_blocks.1.b0
  1.9 0.0 copy-start
  1.9 1.3 %constant_dynamic-slice_fusion = (bf16[2,832,128]{2,1,0:T(8,128)(2,1)S(1)}, bf16[2,832,128]{2,1,0:T(8,128)(2,1)S(1)}) fusion(bf16[2,936,128]{2,1,0:T(8,128)(2,1)} %bitcast.19, s32[]{:T(128)S(6)} %select_n.15, s32[]{:T(128)S(6)} %select_n.14), kind=kLoop, calls=%fused_computation | loop fusion | bytes 1703944 | tf_op jit(solution)/shard_map/dynamic_slice | solution.py:243
  3.2 15.1 %collective-permute-start.3 = (bf16[1664,128]{1,0:T(8,128)(2,1)S(1)}, bf16[1664,128]{1,0:T(8,128)(2,1)S(1)}, u32[]{:S(2)}, u32[]{:S(2)}) collective-permute-start(bf16[1664,128]{1,0:T(8,128)(2,1)S(1)} %bitcast.28), channel_id=1, source_target_pairs={{0,508},{4,8},{8,4},{12,16},{16,12},{20,24},{24,20},{28,32},{32,28... | collective-permute-start | bytes 1277960 | tf_op jit(solution)/shard_map/ppermute | solution.py:221
  18.4 1.9 %collective-permute-start.4 = (bf16[1664,128]{1,0:T(8,128)(2,1)S(1)}, bf16[1664,128]{1,0:T(8,128)(2,1)S(1)}, u32[]{:S(2)}, u32[]{:S(2)}) collective-permute-start(bf16[1664,128]{1,0:T(8,128)(2,1)S(1)} %bitcast.27), channel_id=1, source_target_pairs={{0,4},{4,0},{8,12},{12,8},{16,20},{20,16},{24,28},{28,24},{32,36},... | collective-permute-start | bytes 1277960 | tf_op jit(solution)/shard_map/ppermute | solution.py:222
  20.3 4.8 %collective-permute-start.2 = (bf16[468,128]{1,0:T(8,128)(2,1)S(1)}, bf16[468,128]{1,0:T(8,128)(2,1)S(1)}, u32[]{:S(2)}, u32[]{:S(2)}) collective-permute-start(bf16[468,128]{1,0:T(8,128)(2,1)S(1)} %pack_blocks.1.b0), channel_id=1, source_target_pairs={{0,3},{1,2},{2,1},{3,0},{4,7},{5,6},{6,5},{7,4},{8,11},{9,10},{10,... | collective-permute-start | bytes 359432 | tf_op jit(solution)/shard_map/ppermute | solution.py:239
  25.1 1.9 %collective-permute-start.1 = (bf16[468,128]{1,0:T(8,128)(2,1)S(1)}, bf16[468,128]{1,0:T(8,128)(2,1)S(1)}, u32[]{:S(2)}, u32[]{:S(2)}) collective-permute-start(bf16[468,128]{1,0:T(8,128)(2,1)S(1)} %pack_blocks.1.b0), channel_id=1, source_target_pairs={{0,2},{1,3},{2,0},{3,1},{4,6},{5,7},{6,4},{7,5},{8,10},{9,11},{10,... | collective-permute-start | bytes 359432 | tf_op jit(solution)/shard_map/ppermute | solution.py:239
  27.1 3.4 %collective-permute-start = (bf16[468,128]{1,0:T(8,128)(2,1)S(1)}, bf16[468,128]{1,0:T(8,128)(2,1)S(1)}, u32[]{:S(2)}, u32[]{:S(2)}) collective-permute-start(bf16[468,128]{1,0:T(8,128)(2,1)S(1)} %pack_blocks.1.b0), channel_id=1, source_target_pairs={{0,1},{1,0},{2,3},{3,2},{4,5},{5,4},{6,7},{7,6},{8,9},{9,8},{10,11... | collective-permute-start | bytes 359432 | tf_op jit(solution)/shard_map/ppermute | solution.py:239
  30.4 0.0 copy-start.2
  30.4 0.7 copy-done.2
  31.1 0.0 copy-start.3
  31.2 0.7 copy-done.3
  31.9 0.0 copy-start.4
  31.9 0.7 copy-done.4
  32.5 0.0 copy-start.5
  32.5 0.7 copy-done.5
  33.2 1.1 %trig.1 = (f32[288,128]{1,0:T(8,128)S(1)}, f32[288,128]{1,0:T(8,128)S(1)}, s32[32,36]{1,0:T(8,128)S(1)}) custom-call(f32[2,8]{1,0:T(2,128)S(1)} %bitcast.24, s32[32,36]{1,0:T(8,128)S(1)} %bitcast.22, s32[32,36]{1,0:T(8,128)S(1)} %bitcast.23, s32[1,36]{1,0:T(1,128)S(1)} %bitcast.25), custom_call_target="tpu_custom_call" | custom-call | tf_op jit(solution)/shard_map/trig/pallas_call | solution.py:86
  34.3 0.0 collective-permute-done.2.b3
  34.3 5.4 %collective-permute-done.1.b2 = bf16[468,128]{1,0:T(8,128)(2,1)S(1)} collective-permute-done((bf16[468,128]{1,0:T(8,128)(2,1)S(1)}, bf16[468,128]{1,0:T(8,128)(2,1)S(1)}, u32[]{:S(2)}, u32[]{:S(2)}) %collective-permute-start.1) | collective-permute-done | bytes 119840 | tf_op jit(solution)/shard_map/ppermute | solution.py:239
  39.8 0.0 collective-permute-done.b1
  39.8 0.5 phase_blocks.1.refs_1_
  40.3 0.0 collective-permute-done.3.refs_3_
  40.3 0.0 collective-permute-done.4.refs_4_
  40.3 0.0 copy-done
  40.4 5.7 %apply_blocks.2 = (bf16[1872,128]{1,0:T(8,128)(2,1)S(1)}, bf16[1664,128]{1,0:T(8,128)(2,1)S(1)}, bf16[1664,128]{1,0:T(8,128)(2,1)S(1)}) custom-call(s32[32,36]{1,0:T(8,128)S(1)} %get-tuple-element.10.refs_0_, bf16[2304,512]{1,0:T(8,128)(2,1)S(1)} %phase_blocks.1.refs_1_, bf16[1872,128]{1,0:T(8,128)(2,1)S(1)} %bitcast.20, ...), custom_call_target="tpu_custom_call" | custom-call | tf_op jit(solution)/shard_map/apply_blocks/pallas_call | solution.py:203
  46.0 3.9 %collective-permute-start.5 = (bf16[1664,128]{1,0:T(8,128)(2,1)S(1)}, bf16[1664,128]{1,0:T(8,128)(2,1)S(1)}, u32[]{:S(2)}, u32[]{:S(2)}) collective-permute-start(bf16[1664,128]{1,0:T(8,128)(2,1)S(1)} %get-tuple-element.16), channel_id=1, source_target_pairs={{0,508},{4,8},{8,4},{12,16},{16,12},{20,24},{24,20},{28,32},{32,28... | collective-permute-start | bytes 1277960 | tf_op jit(solution)/shard_map/ppermute | solution.py:221
  49.9 1.9 %collective-permute-start.6 = (bf16[1664,128]{1,0:T(8,128)(2,1)S(1)}, bf16[1664,128]{1,0:T(8,128)(2,1)S(1)}, u32[]{:S(2)}, u32[]{:S(2)}) collective-permute-start(bf16[1664,128]{1,0:T(8,128)(2,1)S(1)} %get-tuple-element.17), channel_id=1, source_target_pairs={{0,4},{4,0},{8,12},{12,8},{16,20},{20,16},{24,28},{28,24},{32,36},... | collective-permute-start | bytes 1277960 | tf_op jit(solution)/shard_map/ppermute | solution.py:222
  51.8 0.8 %copy.8 = bf16[2,36,2,13,128]{4,2,3,1,0:T(2,128)(2,1)} copy(bf16[2,36,2,13,128]{4,2,3,1,0:T(2,128)(2,1)S(1)} %bitcast.18) | data formatting | bytes 958464
  52.6 13.4 %collective-permute-done.5.refs_3_ = bf16[1664,128]{1,0:T(8,128)(2,1)S(1)} collective-permute-done((bf16[1664,128]{1,0:T(8,128)(2,1)S(1)}, bf16[1664,128]{1,0:T(8,128)(2,1)S(1)}, u32[]{:S(2)}, u32[]{:S(2)}) %collective-permute-start.5) | collective-permute-done | bytes 426016 | tf_op jit(solution)/shard_map/ppermute | solution.py:221
  65.9 0.0 collective-permute-done.6.refs_4_
  66.0 6.3 %apply_blocks.3 = bf16[1872,128]{1,0:T(8,128)(2,1)} custom-call(s32[32,36]{1,0:T(8,128)S(1)} %get-tuple-element.10.refs_0_, bf16[2304,512]{1,0:T(8,128)(2,1)S(1)} %phase_blocks.1.refs_1_, bf16[1872,128]{1,0:T(8,128)(2,1)S(1)} %get-tuple-element.15.refs_2_, bf16[1664,128]{1,0:T(8,128)(2,1)S(1)} %collective-permute-done.5.refs_3_, ...), custom_call_target="tpu_custom_call" | custom-call | tf_op jit(solution)/shard_map/apply_blocks/pallas_call | solution.py:203
Async XLA Ops:
  0.6 1.0 %copy-start.1 = (bf16[36,8,13,13]{0,1,3,2:T(8,128)(2,1)S(1)}, bf16[36,8,13,13]{0,1,3,2:T(8,128)(2,1)}, u32[]{:S(2)}) copy-start(bf16[36,8,13,13]{0,1,3,2:T(8,128)(2,1)} %param.6) | copy-start | bytes 292036
  1.9 38.4 %copy-start = (bf16[2,36,2,13,128]{4,2,3,1,0:T(2,128)(2,1)S(1)}, bf16[2,36,2,13,128]{4,2,3,1,0:T(2,128)(2,1)}, u32[]{:S(2)}) copy-start(bf16[2,36,2,13,128]{4,2,3,1,0:T(2,128)(2,1)} %param.7) | copy-start | bytes 1437700
  3.2 37.1 %collective-permute-start.3 = (bf16[1664,128]{1,0:T(8,128)(2,1)S(1)}, bf16[1664,128]{1,0:T(8,128)(2,1)S(1)}, u32[]{:S(2)}, u32[]{:S(2)}) collective-permute-start(bf16[1664,128]{1,0:T(8,128)(2,1)S(1)} %bitcast.28), channel_id=1, source_target_pairs={{0,508},{4,8},{8,4},{12,16},{16,12},{20,24},{24,20},{28,32},{32,28... | collective-permute-start | bytes 1277960 | tf_op jit(solution)/shard_map/ppermute | solution.py:221
  18.4 22.0 %collective-permute-start.4 = (bf16[1664,128]{1,0:T(8,128)(2,1)S(1)}, bf16[1664,128]{1,0:T(8,128)(2,1)S(1)}, u32[]{:S(2)}, u32[]{:S(2)}) collective-permute-start(bf16[1664,128]{1,0:T(8,128)(2,1)S(1)} %bitcast.27), channel_id=1, source_target_pairs={{0,4},{4,0},{8,12},{12,8},{16,20},{20,16},{24,28},{28,24},{32,36},... | collective-permute-start | bytes 1277960 | tf_op jit(solution)/shard_map/ppermute | solution.py:222
  20.3 14.0 %collective-permute-start.2 = (bf16[468,128]{1,0:T(8,128)(2,1)S(1)}, bf16[468,128]{1,0:T(8,128)(2,1)S(1)}, u32[]{:S(2)}, u32[]{:S(2)}) collective-permute-start(bf16[468,128]{1,0:T(8,128)(2,1)S(1)} %pack_blocks.1.b0), channel_id=1, source_target_pairs={{0,3},{1,2},{2,1},{3,0},{4,7},{5,6},{6,5},{7,4},{8,11},{9,10},{10,... | collective-permute-start | bytes 359432 | tf_op jit(solution)/shard_map/ppermute | solution.py:239
  25.1 14.6 %collective-permute-start.1 = (bf16[468,128]{1,0:T(8,128)(2,1)S(1)}, bf16[468,128]{1,0:T(8,128)(2,1)S(1)}, u32[]{:S(2)}, u32[]{:S(2)}) collective-permute-start(bf16[468,128]{1,0:T(8,128)(2,1)S(1)} %pack_blocks.1.b0), channel_id=1, source_target_pairs={{0,2},{1,3},{2,0},{3,1},{4,6},{5,7},{6,4},{7,5},{8,10},{9,11},{10,... | collective-permute-start | bytes 359432 | tf_op jit(solution)/shard_map/ppermute | solution.py:239
  27.1 12.7 %collective-permute-start = (bf16[468,128]{1,0:T(8,128)(2,1)S(1)}, bf16[468,128]{1,0:T(8,128)(2,1)S(1)}, u32[]{:S(2)}, u32[]{:S(2)}) collective-permute-start(bf16[468,128]{1,0:T(8,128)(2,1)S(1)} %pack_blocks.1.b0), channel_id=1, source_target_pairs={{0,1},{1,0},{2,3},{3,2},{4,5},{5,4},{6,7},{7,6},{8,9},{9,8},{10,11... | collective-permute-start | bytes 359432 | tf_op jit(solution)/shard_map/ppermute | solution.py:239
  30.4 0.7 copy-start.2
  31.1 0.7 copy-start.3
  31.9 0.7 copy-start.4
  32.5 0.7 copy-start.5
  46.0 19.9 %collective-permute-start.5 = (bf16[1664,128]{1,0:T(8,128)(2,1)S(1)}, bf16[1664,128]{1,0:T(8,128)(2,1)S(1)}, u32[]{:S(2)}, u32[]{:S(2)}) collective-permute-start(bf16[1664,128]{1,0:T(8,128)(2,1)S(1)} %get-tuple-element.16), channel_id=1, source_target_pairs={{0,508},{4,8},{8,4},{12,16},{16,12},{20,24},{24,20},{28,32},{32,28... | collective-permute-start | bytes 1277960 | tf_op jit(solution)/shard_map/ppermute | solution.py:221
  49.9 16.1 %collective-permute-start.6 = (bf16[1664,128]{1,0:T(8,128)(2,1)S(1)}, bf16[1664,128]{1,0:T(8,128)(2,1)S(1)}, u32[]{:S(2)}, u32[]{:S(2)}) collective-permute-start(bf16[1664,128]{1,0:T(8,128)(2,1)S(1)} %get-tuple-element.17), channel_id=1, source_target_pairs={{0,4},{4,0},{8,12},{12,8},{16,20},{20,16},{24,28},{28,24},{32,36},... | collective-permute-start | bytes 1277960 | tf_op jit(solution)/shard_map/ppermute | solution.py:222
